TPU v7x, 256 devices: a whole 4x4x8 slice. The times are simulated.
256 devices in a mesh: box: 32 (over y_hi, z, core), dir: 8 (over y_lo, x).
Axes of the slice: x: 4, y: 4 (y_hi: 2, y_lo: 2; y = y_hi * 2 + y_lo), z: 8, core: 2. Of those that a mesh axis runs over, the one named last changes fastest.
Arguments:
- leaf_density: bfloat16 [2048, 96, 8, 128], P('box', 'dir'), may hold values from -6 to 6
- phases_first: float32 [8, 96, 64], P(None, 'dir'), may hold values from -3.140625 to 3.140625
- phases_switch: float32 [8, 384, 64], P(None, 'dir'), may hold values from -3.140625 to 3.140625
- phases_top: float32 [8, 1536, 64], P(None, ('box', 'dir')), may hold values from -3.140625 to 3.140625
- transfer_first: bfloat16 [96, 2, 64, 512], P('dir'), may hold values from -0.1875 to 0.1875
- transfer_switch: bfloat16 [384, 2, 64, 512], P('dir'), may hold values from -0.1875 to 0.1875
- transfer_top: bfloat16 [1536, 2, 64, 512], P(('box', 'dir')), may hold values from -0.1875 to 0.1875
- child_mid: int32 [384], P('dir'), may hold values from 0 to 95, as said below
- child_top: int32 [1536], replicated, may hold values from 0 to 383, as said below
Outputs:
- top_density: float32 [4, 1536, 8, 128], P(None, ('box', 'dir'))
Inputs may be any that keep to these rules, and one draw needn't show every extreme that they name: `child_mid`: each level-1 wedge contains exactly 4 level-2 wedges. Each level-2 wedge contains exactly 4 level-3 wedges; with j = (w // 6) mod 8, child_top[w] lies in the level-2 wedges j * 48 to (j + 1) * 48 - 1.
All inputs are finite; a program needn't handle non-finite values.
Results may differ from a plain program's by a relative error of at most 0.0064.
Values may be sent and summed in bfloat16 or wider, within the bound.
No kernel may reach another device: no remote copies, remote signals or barrier semaphores. Data moves between devices by JAX's collectives and lax.ppermute only.
A program may use at most 64 MiB of HBM per device.

v0:
```python
import functools

import jax
import jax.numpy as jnp
from jax import lax
from jax.experimental import pallas as pl
from jax.experimental.pallas import tpu as pltpu
from jax.sharding import PartitionSpec as P


HALF = 64
LANES = 128
EXC = 8
FULL = 8 * HALF
STEP_FIRST = 3
BATCH = 8
X_RING = 4
Y_PAIR = 2
OFFSETS = ((0, 0), (1, 0), (0, 1), (0, -1), (0, 2), (1, 1), (1, -1), (1, 2))


def sin_cos(angle):
    turns = jnp.floor(angle * 0.6366197723675814 + 0.5)
    rest = angle - turns * 1.5703125
    rest = rest - turns * 4.837512969970703e-4
    rest = rest - turns * 7.549789948768648e-8
    square = rest * rest
    sine = rest + rest * square * (
        -1.6666654611e-1 + square * (8.3321608736e-3 - square * 1.9515295891e-4)
    )
    cosine = 1.0 - 0.5 * square + square * square * (
        4.166664568298827e-2 + square * (-1.388731625493765e-3 + square * 2.443315711809948e-5)
    )
    quarter = turns.astype(jnp.int32) & 3
    swap = (quarter & 1) == 1
    sine_abs = jnp.where(swap, cosine, sine)
    cosine_abs = jnp.where(swap, sine, cosine)
    sine_out = jnp.where(quarter >= 2, -sine_abs, sine_abs)
    cosine_out = jnp.where((quarter == 1) | (quarter == 2), -cosine_abs, cosine_abs)
    return sine_out, cosine_out


def left_lanes():
    return lax.broadcasted_iota(jnp.int32, (EXC, LANES), 1) < HALF


def flip(value):
    return pltpu.roll(value, HALF, 1)


def pair_up(first, second, left):
    real = jnp.where(left, first, flip(second))
    imag = jnp.where(left, flip(first), second)
    return real, imag


def turned(real, imag, cosine, sine):
    return jnp.concatenate(
        [cosine * real - sine * imag, sine * real + cosine * imag], axis=0
    ).astype(jnp.bfloat16)


def product(rows, weights):
    return lax.dot_general(
        rows, weights, (((1,), (1,)), ((), ())), preferred_element_type=jnp.float32
    )


def joined(real_rows, imag_rows, left):
    moved = flip(imag_rows)
    return real_rows + jnp.where(left, -moved, moved)


def in_hbm(value):
    return pltpu.with_memory_space_constraint(value, pltpu.HBM)


def fill_trig(trig, angle_of):
    for group in range(4):
        cut = slice(group * LANES, (group + 1) * LANES)
        angle = jnp.concatenate([angle_of(2 * group), angle_of(2 * group + 1)], axis=1)
        trig[0, :, cut], trig[1, :, cut] = sin_cos(angle)


def first_kernel(leaf_hbm, angles_hbm, weights_hbm, out, leaf, angles, weights, rows, trig, sems):
    left = left_lanes()
    wedges = leaf.shape[1]
    steps = wedges // STEP_FIRST

    def copies(step):
        part = pl.ds(step * STEP_FIRST, STEP_FIRST)
        return (
            pltpu.make_async_copy(leaf_hbm.at[:, part], leaf.at[:, part], sems.at[0, step]),
            pltpu.make_async_copy(weights_hbm.at[part], weights.at[part], sems.at[1, step]),
        )

    angle_copy = pltpu.make_async_copy(angles_hbm, angles, sems.at[0, steps])
    angle_copy.start()
    for step in range(steps):
        for copy in copies(step):
            copy.start()
    angle_copy.wait()
    fill_trig(trig, lambda child: angles[:, child, :])
    for wedge in range(wedges):
        if wedge % STEP_FIRST == 0:
            for copy in copies(wedge // STEP_FIRST):
                copy.wait()
        sine = trig[0, wedge : wedge + 1, :]
        cosine = trig[1, wedge : wedge + 1, :]
        place = wedge % 2
        for parent in range(8):
            for group in range(4):
                cut = slice(group * LANES, (group + 1) * LANES)
                child = 8 * parent + 2 * group
                real, imag = pair_up(
                    leaf[child, wedge].astype(jnp.float32),
                    leaf[child + 1, wedge].astype(jnp.float32),
                    left,
                )
                rows[place, parent * 16 : parent * 16 + 16, cut] = turned(real, imag, cosine[:, cut], sine[:, cut])
        result = product(rows[place], weights[wedge])
        pieces = [
            joined(result[16 * p : 16 * p + 8], result[16 * p + 8 : 16 * p + 16], left)
            for p in range(8)
        ]
        for group in range(4):
            real, imag = pair_up(pieces[2 * group], pieces[2 * group + 1], left)
            out[wedge, :, group * LANES : (group + 1) * LANES] = jnp.concatenate([real, imag], axis=0).astype(jnp.bfloat16)


def first_level(leaf, angles, weights):
    wedges = leaf.shape[1]
    hbm = pl.BlockSpec(memory_space=pltpu.HBM)
    return pl.pallas_call(
        first_kernel,
        out_shape=jax.ShapeDtypeStruct((wedges, 16, FULL), jnp.bfloat16),
        in_specs=[hbm, hbm, hbm],
        scratch_shapes=[
            pltpu.VMEM(leaf.shape, jnp.bfloat16),
            pltpu.VMEM(angles.shape, jnp.float32),
            pltpu.VMEM(weights.shape, jnp.bfloat16),
            pltpu.VMEM((2, 128, FULL), jnp.bfloat16),
            pltpu.VMEM((2, wedges, FULL), jnp.float32),
            pltpu.SemaphoreType.DMA((2, wedges // STEP_FIRST + 1)),
        ],
        compiler_params=pltpu.CompilerParams(vmem_limit_bytes=12 << 20),
        name="first_level",
    )(in_hbm(leaf), in_hbm(angles), in_hbm(weights))


def ready_kernel(switch_hbm, top_hbm, weights_hbm, after, switch_trig, top_trig, weights, switch_angles, top_angles, sems):
    weight_copy = pltpu.make_async_copy(weights_hbm, weights, sems.at[0])
    switch_copy = pltpu.make_async_copy(switch_hbm, switch_angles, sems.at[1])
    top_copy = pltpu.make_async_copy(top_hbm, top_angles, sems.at[2])
    switch_copy.start()
    top_copy.start()
    weight_copy.start()
    switch_copy.wait()
    fill_trig(switch_trig, lambda child: switch_angles[child])
    top_copy.wait()
    fill_trig(top_trig, lambda child: top_angles[:, child, :])
    weight_copy.wait()


def make_ready(switch_angles, top_angles, weights, after):
    hbm = pl.BlockSpec(memory_space=pltpu.HBM)
    vmem = pl.BlockSpec(memory_space=pltpu.VMEM)
    return pl.pallas_call(
        ready_kernel,
        out_shape=(
            pltpu.VMEM((2, weights.shape[0], FULL), jnp.float32),
            pltpu.VMEM((2, top_angles.shape[0], FULL), jnp.float32),
            pltpu.VMEM(weights.shape, jnp.bfloat16),
        ),
        in_specs=[hbm, hbm, hbm, pl.BlockSpec(memory_space=pl.ANY)],
        out_specs=(vmem, vmem, vmem),
        scratch_shapes=[
            pltpu.VMEM(switch_angles.shape, jnp.float32),
            pltpu.VMEM(top_angles.shape, jnp.float32),
            pltpu.SemaphoreType.DMA((3,)),
        ],
        compiler_params=pltpu.CompilerParams(vmem_limit_bytes=4 << 20),
        name="make_ready",
    )(in_hbm(switch_angles), in_hbm(top_angles), in_hbm(weights), after)


def lift_one(picked, trig, weights, wedge, left):
    rows = picked.astype(jnp.float32)
    sine = trig[0, pl.ds(wedge, 1), :]
    cosine = trig[1, pl.ds(wedge, 1), :]
    result = product(turned(rows[:8], rows[8:], cosine, sine), weights[wedge])
    return joined(result[:8], result[8:], left).astype(jnp.bfloat16)


def most_kernel(top_count, child_mid, child_top, *refs):
    blocks = refs[:7]
    trig, weights, level_two, plan, gathered = refs[7:]
    left = left_lanes()
    low = gathered.shape[0] // 8
    mid_count = level_two.shape[0]
    slots = plan.shape[0] - 4 * mid_count
    share = lax.axis_index("dir").astype(jnp.int32)
    ahead = 1 - 2 * (lax.axis_index("box").astype(jnp.int32) & 1)
    row, column = share >> 2, share & (X_RING - 1)

    def first_wedge(up, right):
        return low * (((row + up) & 1) * X_RING + ((column - right * ahead) & (X_RING - 1)))

    far = first_wedge(*OFFSETS[7])

    for k in range(7):
        base = first_wedge(*OFFSETS[k])
        for i in range(low):
            gathered[base + i] = blocks[k][i]

    for wedge in range(mid_count):
        source = child_mid[wedge]
        is_far = (source >= far) & (source < far + low)
        picked = gathered[jnp.where(is_far, share * low, source)]
        level_two[wedge] = lift_one(picked, trig, weights, wedge, left)

    def note(wedge, count):
        row = child_mid[wedge] - far
        plan[slots + count] = wedge
        plan[slots + mid_count + count] = row
        return count + jnp.where((row >= 0) & (row < low), 1, 0)

    count = lax.fori_loop(0, mid_count, note, jnp.int32(0))
    plan[slots + 2 * mid_count] = count

    def pad(i, carry):
        plan[slots + i] = plan[slots]
        plan[slots + mid_count + i] = plan[slots + mid_count]
        return carry

    lax.fori_loop(count, mid_count, pad, 0)

    def place(device, carry):
        for slot in range(top_count):
            top = (device * 8 + share) * top_count + slot
            plan[device * top_count + slot] = child_top[top] - share * mid_count
        return carry

    lax.fori_loop(0, slots // top_count, place, 0)


def switch_most(child_mid, child_top, blocks, trig, weights, top_count):
    mid_count = weights.shape[0]
    low = blocks[0].shape[0]
    smem = pl.BlockSpec(memory_space=pltpu.SMEM)
    vmem = pl.BlockSpec(memory_space=pltpu.VMEM)
    return pl.pallas_call(
        functools.partial(most_kernel, top_count),
        out_shape=(
            pltpu.VMEM((mid_count, EXC, LANES), jnp.bfloat16),
            jax.ShapeDtypeStruct((child_top.shape[0] // 8 + 4 * mid_count,), jnp.int32),
        ),
        in_specs=[smem] * 2 + [vmem] * 9,
        out_specs=(vmem, smem),
        scratch_shapes=[pltpu.VMEM((8 * low, 16, FULL), jnp.bfloat16)],
        compiler_params=pltpu.CompilerParams(vmem_limit_bytes=8 << 20),
        name="switch_most",
    )(child_mid, child_top, *blocks, trig, weights)


def rest_kernel(plan, block, trig, weights, ready, out, level_two):
    left = left_lanes()
    mid_count = level_two.shape[0]
    slots = plan.shape[0] - 4 * mid_count
    for wedge in range(mid_count):
        level_two[wedge] = ready[wedge]

    def batch(step, carry):
        for i in range(BATCH):
            wedge = plan[slots + step * BATCH + i]
            row = plan[slots + mid_count + step * BATCH + i]
            level_two[wedge] = lift_one(block[row], trig, weights, wedge, left)
        return carry

    lax.fori_loop(0, (plan[slots + 2 * mid_count] + BATCH - 1) // BATCH, batch, 0)
    top_count = out.shape[1]
    for slot in range(slots):
        out[slot // top_count, slot % top_count] = level_two[plan[slot]]


def switch_rest(plan, block, trig, weights, ready, devices):
    mid_count = weights.shape[0]
    slots = plan.shape[0] - 4 * mid_count
    vmem = pl.BlockSpec(memory_space=pltpu.VMEM)
    return pl.pallas_call(
        rest_kernel,
        out_shape=jax.ShapeDtypeStruct((devices, slots // devices, EXC, LANES), jnp.bfloat16),
        in_specs=[pl.BlockSpec(memory_space=pltpu.SMEM)] + [vmem] * 4,
        scratch_shapes=[pltpu.VMEM((mid_count, EXC, LANES), jnp.bfloat16)],
        compiler_params=pltpu.CompilerParams(vmem_limit_bytes=4 << 20),
        name="switch_rest",
    )(plan, block, trig, weights, ready)


def top_kernel(boxes, trig, weights, out, rows):
    left = left_lanes()
    wedges = weights.shape[0]
    for wedge in range(wedges):
        sine = trig[0, pl.ds(wedge, 1), :]
        cosine = trig[1, pl.ds(wedge, 1), :]
        for parent in range(4):
            for group in range(4):
                cut = slice(group * LANES, (group + 1) * LANES)
                child = 8 * parent + 2 * group
                real, imag = pair_up(
                    boxes[child, wedge].astype(jnp.float32),
                    boxes[child + 1, wedge].astype(jnp.float32),
                    left,
                )
                rows[wedge, parent * 16 : parent * 16 + 16, cut] = turned(real, imag, cosine[:, cut], sine[:, cut])
        result = product(rows[wedge], weights[wedge])
        for p in range(4):
            out[p, wedge] = joined(result[16 * p : 16 * p + 8], result[16 * p + 8 : 16 * p + 16], left)


def top_level(boxes, trig, weights):
    wedges = weights.shape[0]
    return pl.pallas_call(
        top_kernel,
        out_shape=jax.ShapeDtypeStruct((4, wedges, EXC, LANES), jnp.float32),
        scratch_shapes=[
            pltpu.VMEM((wedges, 64, FULL), jnp.bfloat16),
        ],
        compiler_params=pltpu.CompilerParams(vmem_limit_bytes=16 << 20),
        name="top_level",
    )(boxes, trig, weights)


def upward(
    leaf_density,
    phases_first,
    phases_switch,
    phases_top,
    transfer_first,
    transfer_switch,
    transfer_top,
    child_mid,
    child_top,
):
    def flat(weights):
        return weights.reshape(weights.shape[0], LANES, FULL)

    level_one = first_level(leaf_density, phases_first.transpose(1, 0, 2), flat(transfer_first))
    boxes = lax.axis_size("box")

    def moves(up, right):
        pairs = []
        for b in range(boxes):
            for y in range(Y_PAIR):
                for x in range(X_RING):
                    side = right if b % 2 == 0 else -right
                    to_y, to_x = (y + up) % Y_PAIR, (x + side) % X_RING
                    pairs.append(((b * Y_PAIR + y) * X_RING + x, (b * Y_PAIR + to_y) * X_RING + to_x))
        return pairs

    def shift(block, up, right):
        return lax.ppermute(block, ("box", "dir"), moves(up, right))

    other = shift(level_one, 1, 0)
    front = shift(level_one, 0, 1)
    back = shift(level_one, 0, -1)
    far = shift(front, 0, 1)
    other_front = shift(other, 0, 1)
    other_back = shift(back, 1, 0)
    other_far = shift(other_front, 0, 1)
    blocks = (level_one, other, front, back, far, other_front, other_back, other_far)
    switch_trig, top_trig, weights = make_ready(
        phases_switch, phases_top.transpose(1, 0, 2), flat(transfer_switch), level_one
    )
    most, plan = switch_most(
        child_mid, child_top, blocks[:7], switch_trig, weights, transfer_top.shape[0]
    )
    send = switch_rest(plan, other_far, switch_trig, weights, most, boxes)
    received = lax.all_to_all(send, "box", 0, 0)
    return top_level(received, top_trig, flat(transfer_top))


def solution(mesh):
    placed = (
        P("box", "dir", None, None),
        P(None, "dir", None),
        P(None, "dir", None),
        P(None, ("box", "dir"), None),
        P("dir", None, None, None),
        P("dir", None, None, None),
        P(("box", "dir"), None, None, None),
        P("dir"),
        P(),
    )
    return jax.shard_map(
        upward,
        mesh=mesh,
        in_specs=placed,
        out_specs=P(None, ("box", "dir"), None, None),
        check_vma=False,
    )
```

profile of v0, /device:TPU:6, one launch (start us, length us, event | category | flops | bytes accessed | tf_op | source)
XLA Modules:
  0.0 56.3 jit_solution(16251218056051820110)
XLA Ops:
  0.0 0.0 copy-start.2
  0.0 0.0 copy-start.1
  0.0 3.5 %first_level.1.after.refs_0_ = bf16[12,16,512]{2,1,0:T(8,128)(2,1)S(1)} custom-call(bf16[64,12,8,128]{3,2,1,0:T(8,128)(2,1)} %leaf_hbm.1, f32[12,8,64]{2,1,0:T(8,128)} %bitcast.8, bf16[12,128,512]{2,1,0:T(8,128)(2,1)} %bitcast.7), custom_call_target="tpu_custom_call" | custom-call | tf_op jit(solution)/shard_map/first_level/pallas_call | solution.py:134
  3.5 1.7 %collective-permute-start = (bf16[12,16,512]{2,1,0:T(8,128)(2,1)S(1)}, bf16[12,16,512]{2,1,0:T(8,128)(2,1)S(1)}, u32[]{:S(2)}, u32[]{:S(2)}) collective-permute-start(bf16[12,16,512]{2,1,0:T(8,128)(2,1)S(1)} %first_level.1.after.refs_0_), channel_id=1, source_target_pairs={{0,4},{1,5},{2,6},{3,7},{4,0},{5,1},{6,2},{7,3},{8,12},{9,13},{10,... | collective-permute-start | bytes 589832 | tf_op jit(solution)/shard_map/ppermute | solution.py:362
  5.1 0.7 %collective-permute-start.1 = (bf16[12,16,512]{2,1,0:T(8,128)(2,1)S(1)}, bf16[12,16,512]{2,1,0:T(8,128)(2,1)S(1)}, u32[]{:S(2)}, u32[]{:S(2)}) collective-permute-start(bf16[12,16,512]{2,1,0:T(8,128)(2,1)S(1)} %first_level.1.after.refs_0_), channel_id=1, source_target_pairs={{0,1},{1,2},{2,3},{3,0},{4,5},{5,6},{6,7},{7,4},{8,11},{9,8},{10,9... | collective-permute-start | bytes 589832 | tf_op jit(solution)/shard_map/ppermute | solution.py:362
  5.8 1.3 %collective-permute-start.2 = (bf16[12,16,512]{2,1,0:T(8,128)(2,1)S(1)}, bf16[12,16,512]{2,1,0:T(8,128)(2,1)S(1)}, u32[]{:S(2)}, u32[]{:S(2)}) collective-permute-start(bf16[12,16,512]{2,1,0:T(8,128)(2,1)S(1)} %first_level.1.after.refs_0_), channel_id=1, source_target_pairs={{0,3},{1,0},{2,1},{3,2},{4,7},{5,4},{6,5},{7,6},{8,9},{9,10},{10,1... | collective-permute-start | bytes 589832 | tf_op jit(solution)/shard_map/ppermute | solution.py:362
  7.2 3.0 %collective-permute-done.refs_1_ = bf16[12,16,512]{2,1,0:T(8,128)(2,1)S(1)} collective-permute-done((bf16[12,16,512]{2,1,0:T(8,128)(2,1)S(1)}, bf16[12,16,512]{2,1,0:T(8,128)(2,1)S(1)}, u32[]{:S(2)}, u32[]{:S(2)}) %collective-permute-start) | collective-permute-done | bytes 196640 | tf_op jit(solution)/shard_map/ppermute | solution.py:362
  10.2 1.2 %collective-permute-start.4 = (bf16[12,16,512]{2,1,0:T(8,128)(2,1)S(1)}, bf16[12,16,512]{2,1,0:T(8,128)(2,1)S(1)}, u32[]{:S(2)}, u32[]{:S(2)}) collective-permute-start(bf16[12,16,512]{2,1,0:T(8,128)(2,1)S(1)} %collective-permute-done.refs_1_), channel_id=1, source_target_pairs={{0,1},{1,2},{2,3},{3,0},{4,5},{5,6},{6,7},{7,4},{8,11},{9,8},{10,9... | collective-permute-start | bytes 589832 | tf_op jit(solution)/shard_map/ppermute | solution.py:362
  11.4 0.6 %collective-permute-done.1.refs_2_ = bf16[12,16,512]{2,1,0:T(8,128)(2,1)S(1)} collective-permute-done((bf16[12,16,512]{2,1,0:T(8,128)(2,1)S(1)}, bf16[12,16,512]{2,1,0:T(8,128)(2,1)S(1)}, u32[]{:S(2)}, u32[]{:S(2)}) %collective-permute-start.1) | collective-permute-done | bytes 196640 | tf_op jit(solution)/shard_map/ppermute | solution.py:362
  12.1 1.9 %collective-permute-start.3 = (bf16[12,16,512]{2,1,0:T(8,128)(2,1)S(1)}, bf16[12,16,512]{2,1,0:T(8,128)(2,1)S(1)}, u32[]{:S(2)}, u32[]{:S(2)}) collective-permute-start(bf16[12,16,512]{2,1,0:T(8,128)(2,1)S(1)} %collective-permute-done.1.refs_2_), channel_id=1, source_target_pairs={{0,1},{1,2},{2,3},{3,0},{4,5},{5,6},{6,7},{7,4},{8,11},{9,8},{10,9... | collective-permute-start | bytes 589832 | tf_op jit(solution)/shard_map/ppermute | solution.py:362
  14.0 0.0 collective-permute-done.2.refs_3_
  14.0 2.1 %collective-permute-start.5 = (bf16[12,16,512]{2,1,0:T(8,128)(2,1)S(1)}, bf16[12,16,512]{2,1,0:T(8,128)(2,1)S(1)}, u32[]{:S(2)}, u32[]{:S(2)}) collective-permute-start(bf16[12,16,512]{2,1,0:T(8,128)(2,1)S(1)} %collective-permute-done.2.refs_3_), channel_id=1, source_target_pairs={{0,4},{1,5},{2,6},{3,7},{4,0},{5,1},{6,2},{7,3},{8,12},{9,13},{10,... | collective-permute-start | bytes 589832 | tf_op jit(solution)/shard_map/ppermute | solution.py:362
  16.1 0.0 collective-permute-done.4.refs_5_
  16.1 2.2 %collective-permute-start.6 = (bf16[12,16,512]{2,1,0:T(8,128)(2,1)S(1)}, bf16[12,16,512]{2,1,0:T(8,128)(2,1)S(1)}, u32[]{:S(2)}, u32[]{:S(2)}) collective-permute-start(bf16[12,16,512]{2,1,0:T(8,128)(2,1)S(1)} %collective-permute-done.4.refs_5_), channel_id=1, source_target_pairs={{0,1},{1,2},{2,3},{3,0},{4,5},{5,6},{6,7},{7,4},{8,11},{9,8},{10,9... | collective-permute-start | bytes 589832 | tf_op jit(solution)/shard_map/ppermute | solution.py:362
  18.3 2.9 %make_ready.1 = (f32[2,48,512]{2,1,0:T(8,128)S(1)}, f32[2,6,512]{2,1,0:T(8,128)S(1)}, bf16[48,128,512]{2,1,0:T(8,128)(2,1)S(1)}) custom-call(f32[8,48,64]{2,1,0:T(8,128)} %switch_hbm.1, f32[6,8,64]{2,1,0:T(8,128)} %bitcast.9, bf16[48,128,512]{2,1,0:T(8,128)(2,1)} %bitcast.6, bf16[12,16,512]{2,1,0:T(8,128)(2,1)S(1)} %first_level.1.after.refs_0_), custom_call_target="tpu_custom_call" | custom-call | tf_op jit(solution)/shard_map/make_ready/pallas_call | solution.py:168
  21.3 0.0 collective-permute-done.3.refs_4_
  21.3 0.0 collective-permute-done.5.refs_6_
  21.3 0.0 copy-done.2
  21.3 0.0 copy-done.1
  21.3 0.0 copy-start
  21.3 4.2 %switch_most.1 = (bf16[48,8,128]{2,1,0:T(8,128)(2,1)S(1)}, s32[384]{0:T(512)S(1)}) custom-call(s32[48]{0:T(128)S(1)} %copy-done.2, s32[1536]{0:T(1024)S(1)} %copy-done.1, bf16[12,16,512]{2,1,0:T(8,128)(2,1)S(1)} %first_level.1.after.refs_0_, bf16[12,16,512]{2,1,0:T(8,128)(2,1)S(1)} %collective-permute-done.refs_1_, ...), custom_call_target="tpu_custom_call" | custom-call | tf_op jit(solution)/shard_map/switch_most/pallas_call | solution.py:252
  25.6 0.0 collective-permute-done.6.block
  25.6 1.6 %switch_rest.1 = bf16[32,6,8,128]{3,2,1,0:T(8,128)(2,1)S(1)} custom-call(s32[384]{0:T(512)S(1)} %get-tuple-element.12.plan, bf16[12,16,512]{2,1,0:T(8,128)(2,1)S(1)} %collective-permute-done.6.block, f32[2,48,512]{2,1,0:T(8,128)S(1)} %get-tuple-element.10.refs_7_.trig, bf16[48,128,512]{2,1,0:T(8,128)(2,1)S(1)} %get-tuple-element.11.refs_8_.weights, ...), custom_call_target="tpu_custom_call" | custom-call | tf_op jit(solution)/shard_map/switch_rest/pallas_call | solution.py:290
  27.2 27.9 %all_to_all.5.boxes = bf16[32,6,8,128]{3,2,1,0:T(8,128)(2,1)S(1)} all-to-all(bf16[32,6,8,128]{3,2,1,0:T(8,128)(2,1)S(1)} %switch_rest.1), channel_id=1, replica_groups=mesh['box'=32,'dir'=8] {'box'}, dimensions={0} | all-to-all | bytes 786432 | tf_op jit(solution)/shard_map/all_to_all | solution.py:379
  55.1 0.0 copy-done
  55.1 1.2 %top_level.1 = f32[4,6,8,128]{3,2,1,0:T(8,128)} custom-call(bf16[32,6,8,128]{3,2,1,0:T(8,128)(2,1)S(1)} %all_to_all.5.boxes, f32[2,6,512]{2,1,0:T(8,128)S(1)} %get-tuple-element.14.trig, bf16[6,128,512]{2,1,0:T(8,128)(2,1)S(1)} %bitcast.5), custom_call_target="tpu_custom_call" | custom-call | tf_op jit(solution)/shard_map/top_level/pallas_call | solution.py:323
Async XLA Ops:
  0.0 21.3 %copy-start.2 = (s32[48]{0:T(128)S(1)}, s32[48]{0:T(128)}, u32[]{:S(2)}) copy-start(s32[48]{0:T(128)} %child_mid.1) | copy-start | bytes 580
  0.0 21.3 %copy-start.1 = (s32[1536]{0:T(1024)S(1)}, s32[1536]{0:T(1024)}, u32[]{:S(2)}) copy-start(s32[1536]{0:T(1024)} %child_top.1) | copy-start | bytes 18436
  3.5 6.7 %collective-permute-start = (bf16[12,16,512]{2,1,0:T(8,128)(2,1)S(1)}, bf16[12,16,512]{2,1,0:T(8,128)(2,1)S(1)}, u32[]{:S(2)}, u32[]{:S(2)}) collective-permute-start(bf16[12,16,512]{2,1,0:T(8,128)(2,1)S(1)} %first_level.1.after.refs_0_), channel_id=1, source_target_pairs={{0,4},{1,5},{2,6},{3,7},{4,0},{5,1},{6,2},{7,3},{8,12},{9,13},{10,... | collective-permute-start | bytes 589832 | tf_op jit(solution)/shard_map/ppermute | solution.py:362
  5.1 6.9 %collective-permute-start.1 = (bf16[12,16,512]{2,1,0:T(8,128)(2,1)S(1)}, bf16[12,16,512]{2,1,0:T(8,128)(2,1)S(1)}, u32[]{:S(2)}, u32[]{:S(2)}) collective-permute-start(bf16[12,16,512]{2,1,0:T(8,128)(2,1)S(1)} %first_level.1.after.refs_0_), channel_id=1, source_target_pairs={{0,1},{1,2},{2,3},{3,0},{4,5},{5,6},{6,7},{7,4},{8,11},{9,8},{10,9... | collective-permute-start | bytes 589832 | tf_op jit(solution)/shard_map/ppermute | solution.py:362
  5.8 8.1 %collective-permute-start.2 = (bf16[12,16,512]{2,1,0:T(8,128)(2,1)S(1)}, bf16[12,16,512]{2,1,0:T(8,128)(2,1)S(1)}, u32[]{:S(2)}, u32[]{:S(2)}) collective-permute-start(bf16[12,16,512]{2,1,0:T(8,128)(2,1)S(1)} %first_level.1.after.refs_0_), channel_id=1, source_target_pairs={{0,3},{1,0},{2,1},{3,2},{4,7},{5,4},{6,5},{7,6},{8,9},{9,10},{10,1... | collective-permute-start | bytes 589832 | tf_op jit(solution)/shard_map/ppermute | solution.py:362
  10.2 5.9 %collective-permute-start.4 = (bf16[12,16,512]{2,1,0:T(8,128)(2,1)S(1)}, bf16[12,16,512]{2,1,0:T(8,128)(2,1)S(1)}, u32[]{:S(2)}, u32[]{:S(2)}) collective-permute-start(bf16[12,16,512]{2,1,0:T(8,128)(2,1)S(1)} %collective-permute-done.refs_1_), channel_id=1, source_target_pairs={{0,1},{1,2},{2,3},{3,0},{4,5},{5,6},{6,7},{7,4},{8,11},{9,8},{10,9... | collective-permute-start | bytes 589832 | tf_op jit(solution)/shard_map/ppermute | solution.py:362
  12.1 9.2 %collective-permute-start.3 = (bf16[12,16,512]{2,1,0:T(8,128)(2,1)S(1)}, bf16[12,16,512]{2,1,0:T(8,128)(2,1)S(1)}, u32[]{:S(2)}, u32[]{:S(2)}) collective-permute-start(bf16[12,16,512]{2,1,0:T(8,128)(2,1)S(1)} %collective-permute-done.1.refs_2_), channel_id=1, source_target_pairs={{0,1},{1,2},{2,3},{3,0},{4,5},{5,6},{6,7},{7,4},{8,11},{9,8},{10,9... | collective-permute-start | bytes 589832 | tf_op jit(solution)/shard_map/ppermute | solution.py:362
  14.0 7.3 %collective-permute-start.5 = (bf16[12,16,512]{2,1,0:T(8,128)(2,1)S(1)}, bf16[12,16,512]{2,1,0:T(8,128)(2,1)S(1)}, u32[]{:S(2)}, u32[]{:S(2)}) collective-permute-start(bf16[12,16,512]{2,1,0:T(8,128)(2,1)S(1)} %collective-permute-done.2.refs_3_), channel_id=1, source_target_pairs={{0,4},{1,5},{2,6},{3,7},{4,0},{5,1},{6,2},{7,3},{8,12},{9,13},{10,... | collective-permute-start | bytes 589832 | tf_op jit(solution)/shard_map/ppermute | solution.py:362
  16.1 9.4 %collective-permute-start.6 = (bf16[12,16,512]{2,1,0:T(8,128)(2,1)S(1)}, bf16[12,16,512]{2,1,0:T(8,128)(2,1)S(1)}, u32[]{:S(2)}, u32[]{:S(2)}) collective-permute-start(bf16[12,16,512]{2,1,0:T(8,128)(2,1)S(1)} %collective-permute-done.4.refs_5_), channel_id=1, source_target_pairs={{0,1},{1,2},{2,3},{3,0},{4,5},{5,6},{6,7},{7,4},{8,11},{9,8},{10,9... | collective-permute-start | bytes 589832 | tf_op jit(solution)/shard_map/ppermute | solution.py:362
  21.3 33.8 %copy-start = (bf16[6,2,64,512]{3,2,1,0:T(8,128)(2,1)S(1)}, bf16[6,2,64,512]{3,2,1,0:T(8,128)(2,1)}, u32[]{:S(2)}) copy-start(bf16[6,2,64,512]{3,2,1,0:T(8,128)(2,1)} %param.15) | copy-start | bytes 2359300
where the time goes:
time: 56.4 us; the launch traced here: 56.3 us
  blocking collectives  27.9 us (49%)
  Pallas kernels  13.5 us (24%)
  starting transfers between devices  11.1 us (20%)
  waiting for transfers between devices  3.68 us (7%)
    all_to_all x1, blocking collectives, upward(): received = lax.all_to_all(send, 'box', 0, 0)  27.9 us
    ppermute x7, starting transfers between devices, shift(): return lax.ppermute(block, ('box', 'dir'), moves(up, right))  11.1 us
    pallas_call x1, Pallas kernels, switch_most(): pl.pallas_call(functools.partial(most_kernel, top_count), out_shape=(pltp...  4.24 us
    ppermute x7, waiting for transfers between devices, shift(): return lax.ppermute(block, ('box', 'dir'), moves(up, right))  3.68 us
    pallas_call x1, Pallas kernels, first_level(): pl.pallas_call(first_kernel, out_shape=jax.ShapeDtypeStruct((wedges, 16,...  3.47 us
    pallas_call x1, Pallas kernels, make_ready(): pl.pallas_call(ready_kernel, out_shape=(pltpu.VMEM((2, weights.shape[0],...  2.94 us
    pallas_call x1, Pallas kernels, switch_rest(): pl.pallas_call(rest_kernel, out_shape=jax.ShapeDtypeStruct((devices, slot...  1.65 us
    pallas_call x1, Pallas kernels, top_level(): pl.pallas_call(top_kernel, out_shape=jax.ShapeDtypeStruct((4, wedges, EXC...  1.19 us
  transfers between devices with their start and end apart: 7, of which 2 were waited for; matrix products, arithmetic and copies ran while one was open for 0% of the time, Pallas kernels for 13%

commit v1 on v0

--- a/solution.py
+++ b/solution.py
@@ -12,7 +12,7 @@
 LANES = 128
 EXC = 8
 FULL = 8 * HALF
-STEP_FIRST = 3
+STEP_FIRST = 6
 BATCH = 8
 X_RING = 4
 Y_PAIR = 2
@@ -82,7 +82,7 @@
         trig[0, :, cut], trig[1, :, cut] = sin_cos(angle)
 
 
-def first_kernel(leaf_hbm, angles_hbm, weights_hbm, out, leaf, angles, weights, rows, trig, sems):
+def first_kernel(leaf_hbm, angles_hbm, weights_hbm, later_hbm, out, later, leaf, angles, weights, rows, trig, sems):
     left = left_lanes()
     wedges = leaf.shape[1]
     steps = wedges // STEP_FIRST
@@ -95,10 +95,12 @@
         )
 
     angle_copy = pltpu.make_async_copy(angles_hbm, angles, sems.at[0, steps])
+    later_copy = pltpu.make_async_copy(later_hbm, later, sems.at[1, steps])
     angle_copy.start()
     for step in range(steps):
         for copy in copies(step):
             copy.start()
+    later_copy.start()
     angle_copy.wait()
     fill_trig(trig, lambda child: angles[:, child, :])
     for wedge in range(wedges):
@@ -126,15 +128,20 @@
         for group in range(4):
             real, imag = pair_up(pieces[2 * group], pieces[2 * group + 1], left)
             out[wedge, :, group * LANES : (group + 1) * LANES] = jnp.concatenate([real, imag], axis=0).astype(jnp.bfloat16)
-
-
-def first_level(leaf, angles, weights):
+    later_copy.wait()
+
+
+def first_level(leaf, angles, weights, later):
     wedges = leaf.shape[1]
     hbm = pl.BlockSpec(memory_space=pltpu.HBM)
     return pl.pallas_call(
         first_kernel,
-        out_shape=jax.ShapeDtypeStruct((wedges, 16, FULL), jnp.bfloat16),
-        in_specs=[hbm, hbm, hbm],
+        out_shape=(
+            pltpu.VMEM((wedges, 16, FULL), jnp.bfloat16),
+            pltpu.VMEM(later.shape, jnp.bfloat16),
+        ),
+        in_specs=[hbm, hbm, hbm, hbm],
+        out_specs=(pl.BlockSpec(memory_space=pltpu.VMEM), pl.BlockSpec(memory_space=pltpu.VMEM)),
         scratch_shapes=[
             pltpu.VMEM(leaf.shape, jnp.bfloat16),
             pltpu.VMEM(angles.shape, jnp.float32),
@@ -145,43 +152,39 @@
         ],
         compiler_params=pltpu.CompilerParams(vmem_limit_bytes=12 << 20),
         name="first_level",
-    )(in_hbm(leaf), in_hbm(angles), in_hbm(weights))
-
-
-def ready_kernel(switch_hbm, top_hbm, weights_hbm, after, switch_trig, top_trig, weights, switch_angles, top_angles, sems):
-    weight_copy = pltpu.make_async_copy(weights_hbm, weights, sems.at[0])
-    switch_copy = pltpu.make_async_copy(switch_hbm, switch_angles, sems.at[1])
-    top_copy = pltpu.make_async_copy(top_hbm, top_angles, sems.at[2])
+    )(in_hbm(leaf), in_hbm(angles), in_hbm(weights), in_hbm(later))
+
+
+def ready_kernel(switch_hbm, top_hbm, after, switch_trig, top_trig, switch_angles, top_angles, sems):
+    switch_copy = pltpu.make_async_copy(switch_hbm, switch_angles, sems.at[0])
+    top_copy = pltpu.make_async_copy(top_hbm, top_angles, sems.at[1])
     switch_copy.start()
     top_copy.start()
-    weight_copy.start()
     switch_copy.wait()
     fill_trig(switch_trig, lambda child: switch_angles[child])
     top_copy.wait()
     fill_trig(top_trig, lambda child: top_angles[:, child, :])
-    weight_copy.wait()
-
-
-def make_ready(switch_angles, top_angles, weights, after):
+
+
+def make_ready(switch_angles, top_angles, after):
     hbm = pl.BlockSpec(memory_space=pltpu.HBM)
     vmem = pl.BlockSpec(memory_space=pltpu.VMEM)
     return pl.pallas_call(
         ready_kernel,
         out_shape=(
-            pltpu.VMEM((2, weights.shape[0], FULL), jnp.float32),
+            pltpu.VMEM((2, switch_angles.shape[1], FULL), jnp.float32),
             pltpu.VMEM((2, top_angles.shape[0], FULL), jnp.float32),
-            pltpu.VMEM(weights.shape, jnp.bfloat16),
         ),
-        in_specs=[hbm, hbm, hbm, pl.BlockSpec(memory_space=pl.ANY)],
-        out_specs=(vmem, vmem, vmem),
+        in_specs=[hbm, hbm, pl.BlockSpec(memory_space=pl.ANY)],
+        out_specs=(vmem, vmem),
         scratch_shapes=[
             pltpu.VMEM(switch_angles.shape, jnp.float32),
             pltpu.VMEM(top_angles.shape, jnp.float32),
-            pltpu.SemaphoreType.DMA((3,)),
+            pltpu.SemaphoreType.DMA((2,)),
         ],
         compiler_params=pltpu.CompilerParams(vmem_limit_bytes=4 << 20),
         name="make_ready",
-    )(in_hbm(switch_angles), in_hbm(top_angles), in_hbm(weights), after)
+    )(in_hbm(switch_angles), in_hbm(top_angles), after)
 
 
 def lift_one(picked, trig, weights, wedge, left):
@@ -213,35 +216,21 @@
         for i in range(low):
             gathered[base + i] = blocks[k][i]
 
+    count = jnp.int32(0)
+    per_wedge = slots // mid_count
     for wedge in range(mid_count):
         source = child_mid[wedge]
-        is_far = (source >= far) & (source < far + low)
+        row = source - far
+        is_far = (row >= 0) & (row < low)
+        plan[slots + count] = wedge
+        plan[slots + mid_count + count] = row
+        count = count + jnp.where(is_far, 1, 0)
         picked = gathered[jnp.where(is_far, share * low, source)]
         level_two[wedge] = lift_one(picked, trig, weights, wedge, left)
-
-    def note(wedge, count):
-        row = child_mid[wedge] - far
-        plan[slots + count] = wedge
-        plan[slots + mid_count + count] = row
-        return count + jnp.where((row >= 0) & (row < low), 1, 0)
-
-    count = lax.fori_loop(0, mid_count, note, jnp.int32(0))
+        for slot in range(per_wedge * wedge, per_wedge * (wedge + 1)):
+            top = (slot // top_count * 8 + share) * top_count + slot % top_count
+            plan[slot] = child_top[top] - share * mid_count
     plan[slots + 2 * mid_count] = count
-
-    def pad(i, carry):
-        plan[slots + i] = plan[slots]
-        plan[slots + mid_count + i] = plan[slots + mid_count]
-        return carry
-
-    lax.fori_loop(count, mid_count, pad, 0)
-
-    def place(device, carry):
-        for slot in range(top_count):
-            top = (device * 8 + share) * top_count + slot
-            plan[device * top_count + slot] = child_top[top] - share * mid_count
-        return carry
-
-    lax.fori_loop(0, slots // top_count, place, 0)
 
 
 def switch_most(child_mid, child_top, blocks, trig, weights, top_count):
@@ -270,14 +259,17 @@
     for wedge in range(mid_count):
         level_two[wedge] = ready[wedge]
 
+    count = plan[slots + 2 * mid_count]
+
     def batch(step, carry):
         for i in range(BATCH):
-            wedge = plan[slots + step * BATCH + i]
-            row = plan[slots + mid_count + step * BATCH + i]
+            entry = slots + jnp.minimum(step * BATCH + i, count - 1)
+            wedge = plan[entry]
+            row = plan[mid_count + entry]
             level_two[wedge] = lift_one(block[row], trig, weights, wedge, left)
         return carry
 
-    lax.fori_loop(0, (plan[slots + 2 * mid_count] + BATCH - 1) // BATCH, batch, 0)
+    lax.fori_loop(0, (count + BATCH - 1) // BATCH, batch, 0)
     top_count = out.shape[1]
     for slot in range(slots):
         out[slot // top_count, slot % top_count] = level_two[plan[slot]]
@@ -345,7 +337,9 @@
     def flat(weights):
         return weights.reshape(weights.shape[0], LANES, FULL)
 
-    level_one = first_level(leaf_density, phases_first.transpose(1, 0, 2), flat(transfer_first))
+    level_one, weights = first_level(
+        leaf_density, phases_first.transpose(1, 0, 2), flat(transfer_first), flat(transfer_switch)
+    )
     boxes = lax.axis_size("box")
 
     def moves(up, right):
@@ -369,9 +363,7 @@
     other_back = shift(back, 1, 0)
     other_far = shift(other_front, 0, 1)
     blocks = (level_one, other, front, back, far, other_front, other_back, other_far)
-    switch_trig, top_trig, weights = make_ready(
-        phases_switch, phases_top.transpose(1, 0, 2), flat(transfer_switch), level_one
-    )
+    switch_trig, top_trig = make_ready(phases_switch, phases_top.transpose(1, 0, 2), level_one)
     most, plan = switch_most(
         child_mid, child_top, blocks[:7], switch_trig, weights, transfer_top.shape[0]
     )

time: 56.4 us -> 55 us (0.975)
  the two profiles are of different devices: /device:TPU:6 before, /device:TPU:1 now
where the time goes in v1:
time: 55 us; the launch traced here: 54.8 us
  blocking collectives  27.9 us (51%)
  starting transfers between devices  12.7 us (23%)
  Pallas kernels  10.6 us (19%)
  waiting for transfers between devices  3.6 us (7%)
    all_to_all x1, blocking collectives, upward(): received = lax.all_to_all(send, 'box', 0, 0)  27.9 us
    ppermute x7, starting transfers between devices, shift(): return lax.ppermute(block, ('box', 'dir'), moves(up, right))  12.7 us
    pallas_call x1, Pallas kernels, first_level(): pl.pallas_call(first_kernel, out_shape=(pltpu.VMEM((wedges, 16, FULL), jn...  3.85 us
    ppermute x7, waiting for transfers between devices, shift(): return lax.ppermute(block, ('box', 'dir'), moves(up, right))  3.6 us
    pallas_call x1, Pallas kernels, switch_most(): pl.pallas_call(functools.partial(most_kernel, top_count), out_shape=(pltp...  3.11 us
    pallas_call x1, Pallas kernels, make_ready(): pl.pallas_call(ready_kernel, out_shape=(pltpu.VMEM((2, switch_angles.shap...  1.25 us
    pallas_call x1, Pallas kernels, top_level(): pl.pallas_call(top_kernel, out_shape=jax.ShapeDtypeStruct((4, wedges, EXC...  1.19 us
    pallas_call x1, Pallas kernels, switch_rest(): pl.pallas_call(rest_kernel, out_shape=jax.ShapeDtypeStruct((devices, slot...  1.18 us
  transfers between devices with their start and end apart: 7, of which 3 were waited for; matrix products, arithmetic and copies ran while one was open for 0% of the time, Pallas kernels for 8%

profile of v1, /device:TPU:1, one launch (start us, length us, event | category | flops | bytes accessed | tf_op | source)
XLA Modules:
  0.0 54.8 jit_solution(3581128007998618433)
XLA Ops:
  0.0 0.0 copy-start.2
  0.0 0.0 copy-start.1
  0.0 3.9 %first_level.1 = (bf16[12,16,512]{2,1,0:T(8,128)(2,1)S(1)}, bf16[48,128,512]{2,1,0:T(8,128)(2,1)S(1)}) custom-call(bf16[64,12,8,128]{3,2,1,0:T(8,128)(2,1)} %leaf_hbm.1, f32[12,8,64]{2,1,0:T(8,128)} %bitcast.8, bf16[12,128,512]{2,1,0:T(8,128)(2,1)} %bitcast.7, bf16[48,128,512]{2,1,0:T(8,128)(2,1)} %bitcast.6), custom_call_target="tpu_custom_call" | custom-call | tf_op jit(solution)/shard_map/first_level/pallas_call | solution.py:137
  3.9 2.2 %collective-permute-start = (bf16[12,16,512]{2,1,0:T(8,128)(2,1)S(1)}, bf16[12,16,512]{2,1,0:T(8,128)(2,1)S(1)}, u32[]{:S(2)}, u32[]{:S(2)}) collective-permute-start(bf16[12,16,512]{2,1,0:T(8,128)(2,1)S(1)} %get-tuple-element.11.after.refs_0_), channel_id=1, source_target_pairs={{0,4},{1,5},{2,6},{3,7},{4,0},{5,1},{6,2},{7,3},{8,12},{9,13},{10,... | collective-permute-start | bytes 589832 | tf_op jit(solution)/shard_map/ppermute | solution.py:356
  6.1 2.5 %collective-permute-start.1 = (bf16[12,16,512]{2,1,0:T(8,128)(2,1)S(1)}, bf16[12,16,512]{2,1,0:T(8,128)(2,1)S(1)}, u32[]{:S(2)}, u32[]{:S(2)}) collective-permute-start(bf16[12,16,512]{2,1,0:T(8,128)(2,1)S(1)} %get-tuple-element.11.after.refs_0_), channel_id=1, source_target_pairs={{0,1},{1,2},{2,3},{3,0},{4,5},{5,6},{6,7},{7,4},{8,11},{9,8},{10,9... | collective-permute-start | bytes 589832 | tf_op jit(solution)/shard_map/ppermute | solution.py:356
  8.5 0.0 collective-permute-start.2
  8.5 1.0 %collective-permute-done.refs_1_ = bf16[12,16,512]{2,1,0:T(8,128)(2,1)S(1)} collective-permute-done((bf16[12,16,512]{2,1,0:T(8,128)(2,1)S(1)}, bf16[12,16,512]{2,1,0:T(8,128)(2,1)S(1)}, u32[]{:S(2)}, u32[]{:S(2)}) %collective-permute-start) | collective-permute-done | bytes 196640 | tf_op jit(solution)/shard_map/ppermute | solution.py:356
  9.5 3.5 %collective-permute-start.4 = (bf16[12,16,512]{2,1,0:T(8,128)(2,1)S(1)}, bf16[12,16,512]{2,1,0:T(8,128)(2,1)S(1)}, u32[]{:S(2)}, u32[]{:S(2)}) collective-permute-start(bf16[12,16,512]{2,1,0:T(8,128)(2,1)S(1)} %collective-permute-done.refs_1_), channel_id=1, source_target_pairs={{0,1},{1,2},{2,3},{3,0},{4,5},{5,6},{6,7},{7,4},{8,11},{9,8},{10,9... | collective-permute-start | bytes 589832 | tf_op jit(solution)/shard_map/ppermute | solution.py:356
  13.0 0.0 collective-permute-done.1.refs_2_
  13.0 1.2 %collective-permute-start.3 = (bf16[12,16,512]{2,1,0:T(8,128)(2,1)S(1)}, bf16[12,16,512]{2,1,0:T(8,128)(2,1)S(1)}, u32[]{:S(2)}, u32[]{:S(2)}) collective-permute-start(bf16[12,16,512]{2,1,0:T(8,128)(2,1)S(1)} %collective-permute-done.1.refs_2_), channel_id=1, source_target_pairs={{0,1},{1,2},{2,3},{3,0},{4,5},{5,6},{6,7},{7,4},{8,11},{9,8},{10,9... | collective-permute-start | bytes 589832 | tf_op jit(solution)/shard_map/ppermute | solution.py:356
  14.3 1.3 %collective-permute-done.2.refs_3_ = bf16[12,16,512]{2,1,0:T(8,128)(2,1)S(1)} collective-permute-done((bf16[12,16,512]{2,1,0:T(8,128)(2,1)S(1)}, bf16[12,16,512]{2,1,0:T(8,128)(2,1)S(1)}, u32[]{:S(2)}, u32[]{:S(2)}) %collective-permute-start.2) | collective-permute-done | bytes 196640 | tf_op jit(solution)/shard_map/ppermute | solution.py:356
  15.5 0.7 %collective-permute-start.5 = (bf16[12,16,512]{2,1,0:T(8,128)(2,1)S(1)}, bf16[12,16,512]{2,1,0:T(8,128)(2,1)S(1)}, u32[]{:S(2)}, u32[]{:S(2)}) collective-permute-start(bf16[12,16,512]{2,1,0:T(8,128)(2,1)S(1)} %collective-permute-done.2.refs_3_), channel_id=1, source_target_pairs={{0,4},{1,5},{2,6},{3,7},{4,0},{5,1},{6,2},{7,3},{8,12},{9,13},{10,... | collective-permute-start | bytes 589832 | tf_op jit(solution)/shard_map/ppermute | solution.py:356
  16.2 0.0 collective-permute-done.4.refs_5_
  16.2 2.6 %collective-permute-start.6 = (bf16[12,16,512]{2,1,0:T(8,128)(2,1)S(1)}, bf16[12,16,512]{2,1,0:T(8,128)(2,1)S(1)}, u32[]{:S(2)}, u32[]{:S(2)}) collective-permute-start(bf16[12,16,512]{2,1,0:T(8,128)(2,1)S(1)} %collective-permute-done.4.refs_5_), channel_id=1, source_target_pairs={{0,1},{1,2},{2,3},{3,0},{4,5},{5,6},{6,7},{7,4},{8,11},{9,8},{10,9... | collective-permute-start | bytes 589832 | tf_op jit(solution)/shard_map/ppermute | solution.py:356
  18.8 1.3 %make_ready.1 = (f32[2,48,512]{2,1,0:T(8,128)S(1)}, f32[2,6,512]{2,1,0:T(8,128)S(1)}) custom-call(f32[8,48,64]{2,1,0:T(8,128)} %switch_hbm.1, f32[6,8,64]{2,1,0:T(8,128)} %bitcast.9, bf16[12,16,512]{2,1,0:T(8,128)(2,1)S(1)} %get-tuple-element.11.after.refs_0_), custom_call_target="tpu_custom_call" | custom-call | tf_op jit(solution)/shard_map/make_ready/pallas_call | solution.py:172
  20.0 0.0 collective-permute-done.3.refs_4_
  20.0 1.4 %collective-permute-done.5.refs_6_ = bf16[12,16,512]{2,1,0:T(8,128)(2,1)S(1)} collective-permute-done((bf16[12,16,512]{2,1,0:T(8,128)(2,1)S(1)}, bf16[12,16,512]{2,1,0:T(8,128)(2,1)S(1)}, u32[]{:S(2)}, u32[]{:S(2)}) %collective-permute-start.5) | collective-permute-done | bytes 196640 | tf_op jit(solution)/shard_map/ppermute | solution.py:356
  21.4 0.0 copy-done.2
  21.4 0.0 copy-done.1
  21.4 0.0 copy-start
  21.4 3.1 %switch_most.1 = (bf16[48,8,128]{2,1,0:T(8,128)(2,1)S(1)}, s32[384]{0:T(512)S(1)}) custom-call(s32[48]{0:T(128)S(1)} %copy-done.2, s32[1536]{0:T(1024)S(1)} %copy-done.1, bf16[12,16,512]{2,1,0:T(8,128)(2,1)S(1)} %get-tuple-element.11.after.refs_0_, bf16[12,16,512]{2,1,0:T(8,128)(2,1)S(1)} %collective-permute-done.refs_1_, ...), custom_call_target="tpu_custom_call" | custom-call | tf_op jit(solution)/shard_map/switch_most/pallas_call | solution.py:241
  24.5 0.0 collective-permute-done.6.block
  24.5 1.2 %switch_rest.1 = bf16[32,6,8,128]{3,2,1,0:T(8,128)(2,1)S(1)} custom-call(s32[384]{0:T(512)S(1)} %get-tuple-element.14.plan, bf16[12,16,512]{2,1,0:T(8,128)(2,1)S(1)} %collective-permute-done.6.block, f32[2,48,512]{2,1,0:T(8,128)S(1)} %get-tuple-element.12.refs_7_.trig, bf16[48,128,512]{2,1,0:T(8,128)(2,1)S(1)} %get-tuple-element.13.refs_8_.weights, ...), custom_call_target="tpu_custom_call" | custom-call | tf_op jit(solution)/shard_map/switch_rest/pallas_call | solution.py:282
  25.7 27.9 %all_to_all.5.boxes = bf16[32,6,8,128]{3,2,1,0:T(8,128)(2,1)S(1)} all-to-all(bf16[32,6,8,128]{3,2,1,0:T(8,128)(2,1)S(1)} %switch_rest.1), channel_id=1, replica_groups=mesh['box'=32,'dir'=8] {'box'}, dimensions={0} | all-to-all | bytes 786432 | tf_op jit(solution)/shard_map/all_to_all | solution.py:371
  53.7 0.0 copy-done
  53.7 1.2 %top_level.1 = f32[4,6,8,128]{3,2,1,0:T(8,128)} custom-call(bf16[32,6,8,128]{3,2,1,0:T(8,128)(2,1)S(1)} %all_to_all.5.boxes, f32[2,6,512]{2,1,0:T(8,128)S(1)} %get-tuple-element.16.trig, bf16[6,128,512]{2,1,0:T(8,128)(2,1)S(1)} %bitcast.5), custom_call_target="tpu_custom_call" | custom-call | tf_op jit(solution)/shard_map/top_level/pallas_call | solution.py:315
Async XLA Ops:
  0.0 21.4 %copy-start.2 = (s32[48]{0:T(128)S(1)}, s32[48]{0:T(128)}, u32[]{:S(2)}) copy-start(s32[48]{0:T(128)} %child_mid.1) | copy-start | bytes 580
  0.0 21.4 %copy-start.1 = (s32[1536]{0:T(1024)S(1)}, s32[1536]{0:T(1024)}, u32[]{:S(2)}) copy-start(s32[1536]{0:T(1024)} %child_top.1) | copy-start | bytes 18436
  3.9 5.7 %collective-permute-start = (bf16[12,16,512]{2,1,0:T(8,128)(2,1)S(1)}, bf16[12,16,512]{2,1,0:T(8,128)(2,1)S(1)}, u32[]{:S(2)}, u32[]{:S(2)}) collective-permute-start(bf16[12,16,512]{2,1,0:T(8,128)(2,1)S(1)} %get-tuple-element.11.after.refs_0_), channel_id=1, source_target_pairs={{0,4},{1,5},{2,6},{3,7},{4,0},{5,1},{6,2},{7,3},{8,12},{9,13},{10,... | collective-permute-start | bytes 589832 | tf_op jit(solution)/shard_map/ppermute | solution.py:356
  6.1 7.0 %collective-permute-start.1 = (bf16[12,16,512]{2,1,0:T(8,128)(2,1)S(1)}, bf16[12,16,512]{2,1,0:T(8,128)(2,1)S(1)}, u32[]{:S(2)}, u32[]{:S(2)}) collective-permute-start(bf16[12,16,512]{2,1,0:T(8,128)(2,1)S(1)} %get-tuple-element.11.after.refs_0_), channel_id=1, source_target_pairs={{0,1},{1,2},{2,3},{3,0},{4,5},{5,6},{6,7},{7,4},{8,11},{9,8},{10,9... | collective-permute-start | bytes 589832 | tf_op jit(solution)/shard_map/ppermute | solution.py:356
  8.5 7.0 %collective-permute-start.2 = (bf16[12,16,512]{2,1,0:T(8,128)(2,1)S(1)}, bf16[12,16,512]{2,1,0:T(8,128)(2,1)S(1)}, u32[]{:S(2)}, u32[]{:S(2)}) collective-permute-start(bf16[12,16,512]{2,1,0:T(8,128)(2,1)S(1)} %get-tuple-element.11.after.refs_0_), channel_id=1, source_target_pairs={{0,3},{1,0},{2,1},{3,2},{4,7},{5,4},{6,5},{7,6},{8,9},{9,10},{10,1... | collective-permute-start | bytes 589832 | tf_op jit(solution)/shard_map/ppermute | solution.py:356
  9.5 6.7 %collective-permute-start.4 = (bf16[12,16,512]{2,1,0:T(8,128)(2,1)S(1)}, bf16[12,16,512]{2,1,0:T(8,128)(2,1)S(1)}, u32[]{:S(2)}, u32[]{:S(2)}) collective-permute-start(bf16[12,16,512]{2,1,0:T(8,128)(2,1)S(1)} %collective-permute-done.refs_1_), channel_id=1, source_target_pairs={{0,1},{1,2},{2,3},{3,0},{4,5},{5,6},{6,7},{7,4},{8,11},{9,8},{10,9... | collective-permute-start | bytes 589832 | tf_op jit(solution)/shard_map/ppermute | solution.py:356
  13.0 7.0 %collective-permute-start.3 = (bf16[12,16,512]{2,1,0:T(8,128)(2,1)S(1)}, bf16[12,16,512]{2,1,0:T(8,128)(2,1)S(1)}, u32[]{:S(2)}, u32[]{:S(2)}) collective-permute-start(bf16[12,16,512]{2,1,0:T(8,128)(2,1)S(1)} %collective-permute-done.1.refs_2_), channel_id=1, source_target_pairs={{0,1},{1,2},{2,3},{3,0},{4,5},{5,6},{6,7},{7,4},{8,11},{9,8},{10,9... | collective-permute-start | bytes 589832 | tf_op jit(solution)/shard_map/ppermute | solution.py:356
  15.5 5.9 %collective-permute-start.5 = (bf16[12,16,512]{2,1,0:T(8,128)(2,1)S(1)}, bf16[12,16,512]{2,1,0:T(8,128)(2,1)S(1)}, u32[]{:S(2)}, u32[]{:S(2)}) collective-permute-start(bf16[12,16,512]{2,1,0:T(8,128)(2,1)S(1)} %collective-permute-done.2.refs_3_), channel_id=1, source_target_pairs={{0,4},{1,5},{2,6},{3,7},{4,0},{5,1},{6,2},{7,3},{8,12},{9,13},{10,... | collective-permute-start | bytes 589832 | tf_op jit(solution)/shard_map/ppermute | solution.py:356
  16.2 8.3 %collective-permute-start.6 = (bf16[12,16,512]{2,1,0:T(8,128)(2,1)S(1)}, bf16[12,16,512]{2,1,0:T(8,128)(2,1)S(1)}, u32[]{:S(2)}, u32[]{:S(2)}) collective-permute-start(bf16[12,16,512]{2,1,0:T(8,128)(2,1)S(1)} %collective-permute-done.4.refs_5_), channel_id=1, source_target_pairs={{0,1},{1,2},{2,3},{3,0},{4,5},{5,6},{6,7},{7,4},{8,11},{9,8},{10,9... | collective-permute-start | bytes 589832 | tf_op jit(solution)/shard_map/ppermute | solution.py:356
  21.4 32.3 %copy-start = (bf16[6,2,64,512]{3,2,1,0:T(8,128)(2,1)S(1)}, bf16[6,2,64,512]{3,2,1,0:T(8,128)(2,1)}, u32[]{:S(2)}) copy-start(bf16[6,2,64,512]{3,2,1,0:T(8,128)(2,1)} %param.15) | copy-start | bytes 2359300

commit v2 on v0

--- a/solution.py
+++ b/solution.py
@@ -12,11 +12,13 @@
 LANES = 128
 EXC = 8
 FULL = 8 * HALF
-STEP_FIRST = 3
-BATCH = 8
+STEP_FIRST = 6
+BATCH = 10
+PLAN = 5
 X_RING = 4
 Y_PAIR = 2
-OFFSETS = ((0, 0), (1, 0), (0, 1), (0, -1), (0, 2), (1, 1), (1, -1), (1, 2))
+OFFSETS = ((0, 0), (1, 0), (0, 1), (0, -1), (1, 1), (0, 2), (1, -1), (1, 2))
+SOON = 5
 
 
 def sin_cos(angle):
@@ -133,8 +135,9 @@
     hbm = pl.BlockSpec(memory_space=pltpu.HBM)
     return pl.pallas_call(
         first_kernel,
-        out_shape=jax.ShapeDtypeStruct((wedges, 16, FULL), jnp.bfloat16),
+        out_shape=pltpu.VMEM((wedges, 16, FULL), jnp.bfloat16),
         in_specs=[hbm, hbm, hbm],
+        out_specs=pl.BlockSpec(memory_space=pltpu.VMEM),
         scratch_shapes=[
             pltpu.VMEM(leaf.shape, jnp.bfloat16),
             pltpu.VMEM(angles.shape, jnp.float32),
@@ -148,10 +151,15 @@
     )(in_hbm(leaf), in_hbm(angles), in_hbm(weights))
 
 
-def ready_kernel(switch_hbm, top_hbm, weights_hbm, after, switch_trig, top_trig, weights, switch_angles, top_angles, sems):
-    weight_copy = pltpu.make_async_copy(weights_hbm, weights, sems.at[0])
-    switch_copy = pltpu.make_async_copy(switch_hbm, switch_angles, sems.at[1])
-    top_copy = pltpu.make_async_copy(top_hbm, top_angles, sems.at[2])
+def ready_kernel(
+    switch_hbm, top_hbm, weights_hbm, after,
+    switch_trig, top_trig, weights,
+    switch_angles, top_angles, sems,
+):
+    half = pl.ds(0, weights.shape[0] // 2)
+    switch_copy = pltpu.make_async_copy(switch_hbm, switch_angles, sems.at[0])
+    top_copy = pltpu.make_async_copy(top_hbm, top_angles, sems.at[1])
+    weight_copy = pltpu.make_async_copy(weights_hbm.at[half], weights.at[half], sems.at[2])
     switch_copy.start()
     top_copy.start()
     weight_copy.start()
@@ -168,7 +176,7 @@
     return pl.pallas_call(
         ready_kernel,
         out_shape=(
-            pltpu.VMEM((2, weights.shape[0], FULL), jnp.float32),
+            pltpu.VMEM((2, switch_angles.shape[1], FULL), jnp.float32),
             pltpu.VMEM((2, top_angles.shape[0], FULL), jnp.float32),
             pltpu.VMEM(weights.shape, jnp.bfloat16),
         ),
@@ -184,6 +192,28 @@
     )(in_hbm(switch_angles), in_hbm(top_angles), in_hbm(weights), after)
 
 
+def weights_kernel(weights_hbm, after, partial, weights, sem):
+    count = weights.shape[0]
+    half = pl.ds(count // 2, count - count // 2)
+    copy = pltpu.make_async_copy(weights_hbm.at[half], weights.at[half], sem)
+    copy.start()
+    copy.wait()
+
+
+def make_weights(weights, after, partial):
+    vmem = pl.BlockSpec(memory_space=pltpu.VMEM)
+    return pl.pallas_call(
+        weights_kernel,
+        out_shape=pltpu.VMEM(weights.shape, jnp.bfloat16),
+        in_specs=[pl.BlockSpec(memory_space=pltpu.HBM), pl.BlockSpec(memory_space=pl.ANY), vmem],
+        out_specs=vmem,
+        input_output_aliases={2: 0},
+        scratch_shapes=[pltpu.SemaphoreType.DMA],
+        compiler_params=pltpu.CompilerParams(vmem_limit_bytes=1 << 20),
+        name="make_weights",
+    )(in_hbm(weights), after, partial)
+
+
 def lift_one(picked, trig, weights, wedge, left):
     rows = picked.astype(jnp.float32)
     sine = trig[0, pl.ds(wedge, 1), :]
@@ -193,12 +223,12 @@
 
 
 def most_kernel(top_count, child_mid, child_top, *refs):
-    blocks = refs[:7]
-    trig, weights, level_two, plan, gathered = refs[7:]
+    blocks = refs[:SOON]
+    trig, weights, level_two, plan, gathered = refs[SOON:]
     left = left_lanes()
     low = gathered.shape[0] // 8
     mid_count = level_two.shape[0]
-    slots = plan.shape[0] - 4 * mid_count
+    slots = plan.shape[0] - PLAN * mid_count
     share = lax.axis_index("dir").astype(jnp.int32)
     ahead = 1 - 2 * (lax.axis_index("box").astype(jnp.int32) & 1)
     row, column = share >> 2, share & (X_RING - 1)
@@ -206,42 +236,33 @@
     def first_wedge(up, right):
         return low * (((row + up) & 1) * X_RING + ((column - right * ahead) & (X_RING - 1)))
 
-    far = first_wedge(*OFFSETS[7])
-
-    for k in range(7):
+    for k in range(SOON):
         base = first_wedge(*OFFSETS[k])
         for i in range(low):
             gathered[base + i] = blocks[k][i]
 
+    far, side, last = [first_wedge(*offset) for offset in OFFSETS[SOON:]]
+    late = jnp.int32(0)
+    final = jnp.int32(0)
+    per_wedge = slots // mid_count
     for wedge in range(mid_count):
         source = child_mid[wedge]
-        is_far = (source >= far) & (source < far + low)
-        picked = gathered[jnp.where(is_far, share * low, source)]
-        level_two[wedge] = lift_one(picked, trig, weights, wedge, left)
-
-    def note(wedge, count):
-        row = child_mid[wedge] - far
-        plan[slots + count] = wedge
-        plan[slots + mid_count + count] = row
-        return count + jnp.where((row >= 0) & (row < low), 1, 0)
-
-    count = lax.fori_loop(0, mid_count, note, jnp.int32(0))
-    plan[slots + 2 * mid_count] = count
-
-    def pad(i, carry):
-        plan[slots + i] = plan[slots]
-        plan[slots + mid_count + i] = plan[slots + mid_count]
-        return carry
-
-    lax.fori_loop(count, mid_count, pad, 0)
-
-    def place(device, carry):
-        for slot in range(top_count):
-            top = (device * 8 + share) * top_count + slot
-            plan[device * top_count + slot] = child_top[top] - share * mid_count
-        return carry
-
-    lax.fori_loop(0, slots // top_count, place, 0)
+        in_far = (source >= far) & (source < far + low)
+        in_side = (source >= side) & (source < side + low)
+        in_last = (source >= last) & (source < last + low)
+        plan[slots + late] = wedge
+        plan[slots + mid_count + late] = jnp.where(in_far, source - far, source - side + low)
+        late = late + jnp.where(in_far | in_side, 1, 0)
+        plan[slots + 2 * mid_count + final] = wedge
+        plan[slots + 3 * mid_count + final] = source - last
+        final = final + jnp.where(in_last, 1, 0)
+        here = jnp.where(in_far | in_side | in_last, share * low, source)
+        level_two[wedge] = lift_one(gathered[here], trig, weights, wedge, left)
+        for slot in range(per_wedge * wedge, per_wedge * (wedge + 1)):
+            top = (slot // top_count * 8 + share) * top_count + slot % top_count
+            plan[slot] = child_top[top] - share * mid_count
+    plan[slots + 4 * mid_count] = late
+    plan[slots + 4 * mid_count + 1] = final
 
 
 def switch_most(child_mid, child_top, blocks, trig, weights, top_count):
@@ -253,9 +274,9 @@
         functools.partial(most_kernel, top_count),
         out_shape=(
             pltpu.VMEM((mid_count, EXC, LANES), jnp.bfloat16),
-            jax.ShapeDtypeStruct((child_top.shape[0] // 8 + 4 * mid_count,), jnp.int32),
+            jax.ShapeDtypeStruct((child_top.shape[0] // 8 + PLAN * mid_count,), jnp.int32),
         ),
-        in_specs=[smem] * 2 + [vmem] * 9,
+        in_specs=[smem] * 2 + [vmem] * (SOON + 2),
         out_specs=(vmem, smem),
         scratch_shapes=[pltpu.VMEM((8 * low, 16, FULL), jnp.bfloat16)],
         compiler_params=pltpu.CompilerParams(vmem_limit_bytes=8 << 20),
@@ -263,38 +284,68 @@
     )(child_mid, child_top, *blocks, trig, weights)
 
 
-def rest_kernel(plan, block, trig, weights, ready, out, level_two):
+def lift_listed(plan, start, count, rows, trig, weights, level_two):
     left = left_lanes()
     mid_count = level_two.shape[0]
-    slots = plan.shape[0] - 4 * mid_count
+
+    def batch(step, carry):
+        for i in range(BATCH):
+            entry = start + jnp.minimum(step * BATCH + i, count - 1)
+            wedge = plan[entry]
+            level_two[wedge] = lift_one(rows[plan[mid_count + entry]], trig, weights, wedge, left)
+        return carry
+
+    lax.fori_loop(0, (count + BATCH - 1) // BATCH, batch, 0)
+
+
+def late_kernel(plan, far, side, trig, weights, ready, level_two, gathered):
+    mid_count, low = level_two.shape[0], far.shape[0]
+    slots = plan.shape[0] - PLAN * mid_count
     for wedge in range(mid_count):
         level_two[wedge] = ready[wedge]
-
-    def batch(step, carry):
-        for i in range(BATCH):
-            wedge = plan[slots + step * BATCH + i]
-            row = plan[slots + mid_count + step * BATCH + i]
-            level_two[wedge] = lift_one(block[row], trig, weights, wedge, left)
-        return carry
-
-    lax.fori_loop(0, (plan[slots + 2 * mid_count] + BATCH - 1) // BATCH, batch, 0)
+    for i in range(low):
+        gathered[i] = far[i]
+        gathered[low + i] = side[i]
+    lift_listed(plan, slots, plan[slots + 4 * mid_count], gathered, trig, weights, level_two)
+
+
+def switch_late(plan, far, side, trig, weights, ready):
+    vmem = pl.BlockSpec(memory_space=pltpu.VMEM)
+    return pl.pallas_call(
+        late_kernel,
+        out_shape=pltpu.VMEM(ready.shape, jnp.bfloat16),
+        in_specs=[pl.BlockSpec(memory_space=pltpu.SMEM)] + [vmem] * 5,
+        out_specs=vmem,
+        scratch_shapes=[pltpu.VMEM((2 * far.shape[0], 16, FULL), jnp.bfloat16)],
+        compiler_params=pltpu.CompilerParams(vmem_limit_bytes=4 << 20),
+        name="switch_late",
+    )(plan, far, side, trig, weights, ready)
+
+
+def rest_kernel(plan, last, trig, weights, ready, out, level_two):
+    mid_count = level_two.shape[0]
+    slots = plan.shape[0] - PLAN * mid_count
+    for wedge in range(mid_count):
+        level_two[wedge] = ready[wedge]
+    count = plan[slots + 4 * mid_count + 1]
+    lift_listed(plan, slots + 2 * mid_count, count, last, trig, weights, level_two)
     top_count = out.shape[1]
     for slot in range(slots):
         out[slot // top_count, slot % top_count] = level_two[plan[slot]]
 
 
-def switch_rest(plan, block, trig, weights, ready, devices):
+def switch_rest(plan, last, trig, weights, ready, devices):
     mid_count = weights.shape[0]
-    slots = plan.shape[0] - 4 * mid_count
+    slots = plan.shape[0] - PLAN * mid_count
     vmem = pl.BlockSpec(memory_space=pltpu.VMEM)
     return pl.pallas_call(
         rest_kernel,
         out_shape=jax.ShapeDtypeStruct((devices, slots // devices, EXC, LANES), jnp.bfloat16),
         in_specs=[pl.BlockSpec(memory_space=pltpu.SMEM)] + [vmem] * 4,
-        scratch_shapes=[pltpu.VMEM((mid_count, EXC, LANES), jnp.bfloat16)],
+        scratch_shapes=[pltpu.VMEM(ready.shape, jnp.bfloat16)],
         compiler_params=pltpu.CompilerParams(vmem_limit_bytes=4 << 20),
         name="switch_rest",
-    )(plan, block, trig, weights, ready)
+    )(plan, last, trig, weights, ready)
 
 
 def top_kernel(boxes, trig, weights, out, rows):
@@ -368,14 +419,16 @@
     other_front = shift(other, 0, 1)
     other_back = shift(back, 1, 0)
     other_far = shift(other_front, 0, 1)
-    blocks = (level_one, other, front, back, far, other_front, other_back, other_far)
-    switch_trig, top_trig, weights = make_ready(
+    blocks = (level_one, other, front, back, other_front)
+    switch_trig, top_trig, partial = make_ready(
         phases_switch, phases_top.transpose(1, 0, 2), flat(transfer_switch), level_one
     )
+    weights = make_weights(flat(transfer_switch), back, partial)
     most, plan = switch_most(
-        child_mid, child_top, blocks[:7], switch_trig, weights, transfer_top.shape[0]
-    )
-    send = switch_rest(plan, other_far, switch_trig, weights, most, boxes)
+        child_mid, child_top, blocks, switch_trig, weights, transfer_top.shape[0]
+    )
+    late = switch_late(plan, far, other_back, switch_trig, weights, most)
+    send = switch_rest(plan, other_far, switch_trig, weights, late, boxes)
     received = lax.all_to_all(send, "box", 0, 0)
     return top_level(received, top_trig, flat(transfer_top))
 

time: 56.4 us -> 57.6 us (1.021)
  the two profiles are of different devices: /device:TPU:6 before, /device:TPU:2 now
where the time goes in v2:
time: 57.6 us; the launch traced here: 57.4 us
  blocking collectives  28.6 us (50%)
  Pallas kernels  14.8 us (26%)
  starting transfers between devices  8.24 us (14%)
  waiting for transfers between devices  5.66 us (10%)
    all_to_all x1, blocking collectives, upward(): received = lax.all_to_all(send, 'box', 0, 0)  28.6 us
    ppermute x7, starting transfers between devices, shift(): return lax.ppermute(block, ('box', 'dir'), moves(up, right))  8.24 us
    ppermute x7, waiting for transfers between devices, shift(): return lax.ppermute(block, ('box', 'dir'), moves(up, right))  5.66 us
    pallas_call x1, Pallas kernels, switch_most(): pl.pallas_call(functools.partial(most_kernel, top_count), out_shape=(pltp...  3.08 us
    pallas_call x1, Pallas kernels, first_level(): pl.pallas_call(first_kernel, out_shape=pltpu.VMEM((wedges, 16, FULL), jnp...  3.07 us
    pallas_call x1, Pallas kernels, make_ready(): pl.pallas_call(ready_kernel, out_shape=(pltpu.VMEM((2, switch_angles.shap...  2.05 us
    pallas_call x1, Pallas kernels, make_weights(): pl.pallas_call(weights_kernel, out_shape=pltpu.VMEM(weights.shape, jnp.bf...  1.91 us
    pallas_call x1, Pallas kernels, switch_rest(): pl.pallas_call(rest_kernel, out_shape=jax.ShapeDtypeStruct((devices, slot...  1.82 us
  transfers between devices with their start and end apart: 7, of which 3 were waited for; matrix products, arithmetic and copies ran while one was open for 0% of the time, Pallas kernels for 15%

profile of v2, /device:TPU:2, one launch (start us, length us, event | category | flops | bytes accessed | tf_op | source)
XLA Modules:
  0.0 57.4 jit_solution(13983514783591923364)
XLA Ops:
  0.0 3.1 %first_level.1.after.refs_0_ = bf16[12,16,512]{2,1,0:T(8,128)(2,1)S(1)} custom-call(bf16[64,12,8,128]{3,2,1,0:T(8,128)(2,1)} %leaf_hbm.1, f32[12,8,64]{2,1,0:T(8,128)} %bitcast.9, bf16[12,128,512]{2,1,0:T(8,128)(2,1)} %bitcast.8), custom_call_target="tpu_custom_call" | custom-call | tf_op jit(solution)/shard_map/first_level/pallas_call | solution.py:136
  3.1 1.7 %collective-permute-start = (bf16[12,16,512]{2,1,0:T(8,128)(2,1)S(1)}, bf16[12,16,512]{2,1,0:T(8,128)(2,1)S(1)}, u32[]{:S(2)}, u32[]{:S(2)}) collective-permute-start(bf16[12,16,512]{2,1,0:T(8,128)(2,1)S(1)} %first_level.1.after.refs_0_), channel_id=1, source_target_pairs={{0,4},{1,5},{2,6},{3,7},{4,0},{5,1},{6,2},{7,3},{8,12},{9,13},{10,... | collective-permute-start | bytes 589832 | tf_op jit(solution)/shard_map/ppermute | solution.py:413
  4.7 0.8 %collective-permute-start.2 = (bf16[12,16,512]{2,1,0:T(8,128)(2,1)S(1)}, bf16[12,16,512]{2,1,0:T(8,128)(2,1)S(1)}, u32[]{:S(2)}, u32[]{:S(2)}) collective-permute-start(bf16[12,16,512]{2,1,0:T(8,128)(2,1)S(1)} %first_level.1.after.refs_0_), channel_id=1, source_target_pairs={{0,3},{1,0},{2,1},{3,2},{4,7},{5,4},{6,5},{7,6},{8,9},{9,10},{10,1... | collective-permute-start | bytes 589832 | tf_op jit(solution)/shard_map/ppermute | solution.py:413
  5.5 1.3 %collective-permute-start.1 = (bf16[12,16,512]{2,1,0:T(8,128)(2,1)S(1)}, bf16[12,16,512]{2,1,0:T(8,128)(2,1)S(1)}, u32[]{:S(2)}, u32[]{:S(2)}) collective-permute-start(bf16[12,16,512]{2,1,0:T(8,128)(2,1)S(1)} %first_level.1.after.refs_0_), channel_id=1, source_target_pairs={{0,1},{1,2},{2,3},{3,0},{4,5},{5,6},{6,7},{7,4},{8,11},{9,8},{10,9... | collective-permute-start | bytes 589832 | tf_op jit(solution)/shard_map/ppermute | solution.py:413
  6.8 3.0 %collective-permute-done.refs_1_ = bf16[12,16,512]{2,1,0:T(8,128)(2,1)S(1)} collective-permute-done((bf16[12,16,512]{2,1,0:T(8,128)(2,1)S(1)}, bf16[12,16,512]{2,1,0:T(8,128)(2,1)S(1)}, u32[]{:S(2)}, u32[]{:S(2)}) %collective-permute-start) | collective-permute-done | bytes 196640 | tf_op jit(solution)/shard_map/ppermute | solution.py:413
  9.8 1.5 %collective-permute-start.3 = (bf16[12,16,512]{2,1,0:T(8,128)(2,1)S(1)}, bf16[12,16,512]{2,1,0:T(8,128)(2,1)S(1)}, u32[]{:S(2)}, u32[]{:S(2)}) collective-permute-start(bf16[12,16,512]{2,1,0:T(8,128)(2,1)S(1)} %collective-permute-done.refs_1_), channel_id=1, source_target_pairs={{0,1},{1,2},{2,3},{3,0},{4,5},{5,6},{6,7},{7,4},{8,11},{9,8},{10,9... | collective-permute-start | bytes 589832 | tf_op jit(solution)/shard_map/ppermute | solution.py:413
  11.3 1.2 %collective-permute-done.2.after.refs_3_ = bf16[12,16,512]{2,1,0:T(8,128)(2,1)S(1)} collective-permute-done((bf16[12,16,512]{2,1,0:T(8,128)(2,1)S(1)}, bf16[12,16,512]{2,1,0:T(8,128)(2,1)S(1)}, u32[]{:S(2)}, u32[]{:S(2)}) %collective-permute-start.2) | collective-permute-done | bytes 196640 | tf_op jit(solution)/shard_map/ppermute | solution.py:413
  12.5 0.4 collective-permute-start.6
  12.9 0.0 collective-permute-done.1.refs_2_
  12.9 1.2 %collective-permute-start.5 = (bf16[12,16,512]{2,1,0:T(8,128)(2,1)S(1)}, bf16[12,16,512]{2,1,0:T(8,128)(2,1)S(1)}, u32[]{:S(2)}, u32[]{:S(2)}) collective-permute-start(bf16[12,16,512]{2,1,0:T(8,128)(2,1)S(1)} %collective-permute-done.1.refs_2_), channel_id=1, source_target_pairs={{0,1},{1,2},{2,3},{3,0},{4,5},{5,6},{6,7},{7,4},{8,11},{9,8},{10,9... | collective-permute-start | bytes 589832 | tf_op jit(solution)/shard_map/ppermute | solution.py:413
  14.1 1.4 %collective-permute-done.3.refs_4_ = bf16[12,16,512]{2,1,0:T(8,128)(2,1)S(1)} collective-permute-done((bf16[12,16,512]{2,1,0:T(8,128)(2,1)S(1)}, bf16[12,16,512]{2,1,0:T(8,128)(2,1)S(1)}, u32[]{:S(2)}, u32[]{:S(2)}) %collective-permute-start.3) | collective-permute-done | bytes 196640 | tf_op jit(solution)/shard_map/ppermute | solution.py:413
  15.5 1.5 %collective-permute-start.4 = (bf16[12,16,512]{2,1,0:T(8,128)(2,1)S(1)}, bf16[12,16,512]{2,1,0:T(8,128)(2,1)S(1)}, u32[]{:S(2)}, u32[]{:S(2)}) collective-permute-start(bf16[12,16,512]{2,1,0:T(8,128)(2,1)S(1)} %collective-permute-done.3.refs_4_), channel_id=1, source_target_pairs={{0,1},{1,2},{2,3},{3,0},{4,5},{5,6},{6,7},{7,4},{8,11},{9,8},{10,9... | collective-permute-start | bytes 589832 | tf_op jit(solution)/shard_map/ppermute | solution.py:413
  17.0 2.0 %make_ready.1 = (f32[2,48,512]{2,1,0:T(8,128)S(1)}, f32[2,6,512]{2,1,0:T(8,128)S(1)}, bf16[48,128,512]{2,1,0:T(8,128)(2,1)S(1)}) custom-call(f32[8,48,64]{2,1,0:T(8,128)} %switch_hbm.1, f32[6,8,64]{2,1,0:T(8,128)} %bitcast.10, bf16[48,128,512]{2,1,0:T(8,128)(2,1)} %bitcast.6, bf16[12,16,512]{2,1,0:T(8,128)(2,1)S(1)} %first_level.1.after.refs_0_), custom_call_target="tpu_custom_call" | custom-call | tf_op jit(solution)/shard_map/make_ready/pallas_call | solution.py:176
  19.0 0.0 copy-start.1
  19.0 0.0 copy-start.2
  19.1 1.9 %make_weights.1.refs_6_.weights = bf16[48,128,512]{2,1,0:T(8,128)(2,1)S(1)} custom-call(bf16[48,128,512]{2,1,0:T(8,128)(2,1)} %bitcast.7, bf16[12,16,512]{2,1,0:T(8,128)(2,1)S(1)} %collective-permute-done.2.after.refs_3_, bf16[48,128,512]{2,1,0:T(8,128)(2,1)S(1)} %get-tuple-element.11.partial), custom_call_target="tpu_custom_call", output_to_operand_aliasing={{}: (2, {})} | custom-call | tf_op jit(solution)/shard_map/make_weights/pallas_call | solution.py:205
  21.0 0.0 copy-done.1
  21.0 0.0 copy-done.2
  21.0 3.1 %switch_most.1 = (bf16[48,8,128]{2,1,0:T(8,128)(2,1)S(1)}, s32[432]{0:T(512)S(1)}) custom-call(s32[48]{0:T(128)S(1)} %copy-done.2, s32[1536]{0:T(1024)S(1)} %copy-done.1, bf16[12,16,512]{2,1,0:T(8,128)(2,1)S(1)} %first_level.1.after.refs_0_, bf16[12,16,512]{2,1,0:T(8,128)(2,1)S(1)} %collective-permute-done.refs_1_, ...), custom_call_target="tpu_custom_call" | custom-call | tf_op jit(solution)/shard_map/switch_most/pallas_call | solution.py:273
  24.1 0.0 collective-permute-done.6.side
  24.1 0.0 collective-permute-done.5.far
  24.1 0.0 copy-start
  24.1 1.6 %switch_late.1.ready = bf16[48,8,128]{2,1,0:T(8,128)(2,1)S(1)} custom-call(s32[432]{0:T(512)S(1)} %get-tuple-element.12.plan, bf16[12,16,512]{2,1,0:T(8,128)(2,1)S(1)} %collective-permute-done.5.far, bf16[12,16,512]{2,1,0:T(8,128)(2,1)S(1)} %collective-permute-done.6.side, f32[2,48,512]{2,1,0:T(8,128)S(1)} %get-tuple-element.10.refs_5_.trig, ...), custom_call_target="tpu_custom_call" | custom-call | tf_op jit(solution)/shard_map/switch_late/pallas_call | solution.py:314
  25.8 0.0 collective-permute-done.4.last
  25.8 1.8 %switch_rest.1 = bf16[32,6,8,128]{3,2,1,0:T(8,128)(2,1)S(1)} custom-call(s32[432]{0:T(512)S(1)} %get-tuple-element.12.plan, bf16[12,16,512]{2,1,0:T(8,128)(2,1)S(1)} %collective-permute-done.4.last, f32[2,48,512]{2,1,0:T(8,128)S(1)} %get-tuple-element.10.refs_5_.trig, bf16[48,128,512]{2,1,0:T(8,128)(2,1)S(1)} %make_weights.1.refs_6_.weights, ...), custom_call_target="tpu_custom_call" | custom-call | tf_op jit(solution)/shard_map/switch_rest/pallas_call | solution.py:341
  27.6 28.6 %all_to_all.5.boxes = bf16[32,6,8,128]{3,2,1,0:T(8,128)(2,1)S(1)} all-to-all(bf16[32,6,8,128]{3,2,1,0:T(8,128)(2,1)S(1)} %switch_rest.1), channel_id=1, replica_groups=mesh['box'=32,'dir'=8] {'box'}, dimensions={0} | all-to-all | bytes 786432 | tf_op jit(solution)/shard_map/all_to_all | solution.py:432
  56.2 0.0 copy-done
  56.2 1.2 %top_level.1 = f32[4,6,8,128]{3,2,1,0:T(8,128)} custom-call(bf16[32,6,8,128]{3,2,1,0:T(8,128)(2,1)S(1)} %all_to_all.5.boxes, f32[2,6,512]{2,1,0:T(8,128)S(1)} %get-tuple-element.14.trig, bf16[6,128,512]{2,1,0:T(8,128)(2,1)S(1)} %bitcast.5), custom_call_target="tpu_custom_call" | custom-call | tf_op jit(solution)/shard_map/top_level/pallas_call | solution.py:374
Async XLA Ops:
  3.1 6.7 %collective-permute-start = (bf16[12,16,512]{2,1,0:T(8,128)(2,1)S(1)}, bf16[12,16,512]{2,1,0:T(8,128)(2,1)S(1)}, u32[]{:S(2)}, u32[]{:S(2)}) collective-permute-start(bf16[12,16,512]{2,1,0:T(8,128)(2,1)S(1)} %first_level.1.after.refs_0_), channel_id=1, source_target_pairs={{0,4},{1,5},{2,6},{3,7},{4,0},{5,1},{6,2},{7,3},{8,12},{9,13},{10,... | collective-permute-start | bytes 589832 | tf_op jit(solution)/shard_map/ppermute | solution.py:413
  4.7 7.8 %collective-permute-start.2 = (bf16[12,16,512]{2,1,0:T(8,128)(2,1)S(1)}, bf16[12,16,512]{2,1,0:T(8,128)(2,1)S(1)}, u32[]{:S(2)}, u32[]{:S(2)}) collective-permute-start(bf16[12,16,512]{2,1,0:T(8,128)(2,1)S(1)} %first_level.1.after.refs_0_), channel_id=1, source_target_pairs={{0,3},{1,0},{2,1},{3,2},{4,7},{5,4},{6,5},{7,6},{8,9},{9,10},{10,1... | collective-permute-start | bytes 589832 | tf_op jit(solution)/shard_map/ppermute | solution.py:413
  5.5 7.4 %collective-permute-start.1 = (bf16[12,16,512]{2,1,0:T(8,128)(2,1)S(1)}, bf16[12,16,512]{2,1,0:T(8,128)(2,1)S(1)}, u32[]{:S(2)}, u32[]{:S(2)}) collective-permute-start(bf16[12,16,512]{2,1,0:T(8,128)(2,1)S(1)} %first_level.1.after.refs_0_), channel_id=1, source_target_pairs={{0,1},{1,2},{2,3},{3,0},{4,5},{5,6},{6,7},{7,4},{8,11},{9,8},{10,9... | collective-permute-start | bytes 589832 | tf_op jit(solution)/shard_map/ppermute | solution.py:413
  9.8 5.7 %collective-permute-start.3 = (bf16[12,16,512]{2,1,0:T(8,128)(2,1)S(1)}, bf16[12,16,512]{2,1,0:T(8,128)(2,1)S(1)}, u32[]{:S(2)}, u32[]{:S(2)}) collective-permute-start(bf16[12,16,512]{2,1,0:T(8,128)(2,1)S(1)} %collective-permute-done.refs_1_), channel_id=1, source_target_pairs={{0,1},{1,2},{2,3},{3,0},{4,5},{5,6},{6,7},{7,4},{8,11},{9,8},{10,9... | collective-permute-start | bytes 589832 | tf_op jit(solution)/shard_map/ppermute | solution.py:413
  12.5 11.6 %collective-permute-start.6 = (bf16[12,16,512]{2,1,0:T(8,128)(2,1)S(1)}, bf16[12,16,512]{2,1,0:T(8,128)(2,1)S(1)}, u32[]{:S(2)}, u32[]{:S(2)}) collective-permute-start(bf16[12,16,512]{2,1,0:T(8,128)(2,1)S(1)} %collective-permute-done.2.after.refs_3_), channel_id=1, source_target_pairs={{0,4},{1,5},{2,6},{3,7},{4,0},{5,1},{6,2},{7,3},{8,12},{9,13},{10,... | collective-permute-start | bytes 589832 | tf_op jit(solution)/shard_map/ppermute | solution.py:413
  12.9 11.2 %collective-permute-start.5 = (bf16[12,16,512]{2,1,0:T(8,128)(2,1)S(1)}, bf16[12,16,512]{2,1,0:T(8,128)(2,1)S(1)}, u32[]{:S(2)}, u32[]{:S(2)}) collective-permute-start(bf16[12,16,512]{2,1,0:T(8,128)(2,1)S(1)} %collective-permute-done.1.refs_2_), channel_id=1, source_target_pairs={{0,1},{1,2},{2,3},{3,0},{4,5},{5,6},{6,7},{7,4},{8,11},{9,8},{10,9... | collective-permute-start | bytes 589832 | tf_op jit(solution)/shard_map/ppermute | solution.py:413
  15.5 10.3 %collective-permute-start.4 = (bf16[12,16,512]{2,1,0:T(8,128)(2,1)S(1)}, bf16[12,16,512]{2,1,0:T(8,128)(2,1)S(1)}, u32[]{:S(2)}, u32[]{:S(2)}) collective-permute-start(bf16[12,16,512]{2,1,0:T(8,128)(2,1)S(1)} %collective-permute-done.3.refs_4_), channel_id=1, source_target_pairs={{0,1},{1,2},{2,3},{3,0},{4,5},{5,6},{6,7},{7,4},{8,11},{9,8},{10,9... | collective-permute-start | bytes 589832 | tf_op jit(solution)/shard_map/ppermute | solution.py:413
  19.0 1.9 %copy-start.1 = (s32[1536]{0:T(1024)S(1)}, s32[1536]{0:T(1024)}, u32[]{:S(2)}) copy-start(s32[1536]{0:T(1024)} %child_top.1) | copy-start | bytes 18436
  19.0 1.9 %copy-start.2 = (s32[48]{0:T(128)S(1)}, s32[48]{0:T(128)}, u32[]{:S(2)}) copy-start(s32[48]{0:T(128)} %child_mid.1) | copy-start | bytes 580
  24.1 32.1 %copy-start = (bf16[6,2,64,512]{3,2,1,0:T(8,128)(2,1)S(1)}, bf16[6,2,64,512]{3,2,1,0:T(8,128)(2,1)}, u32[]{:S(2)}) copy-start(bf16[6,2,64,512]{3,2,1,0:T(8,128)(2,1)} %param.15) | copy-start | bytes 2359300

commit v3 on v2

--- a/solution.py
+++ b/solution.py
@@ -16,8 +16,6 @@
 BATCH = 10
 PLAN = 5
 X_RING = 4
-Y_PAIR = 2
-OFFSETS = ((0, 0), (1, 0), (0, 1), (0, -1), (1, 1), (0, 2), (1, -1), (1, 2))
 SOON = 5
 
 
@@ -230,18 +228,19 @@
     mid_count = level_two.shape[0]
     slots = plan.shape[0] - PLAN * mid_count
     share = lax.axis_index("dir").astype(jnp.int32)
-    ahead = 1 - 2 * (lax.axis_index("box").astype(jnp.int32) & 1)
-    row, column = share >> 2, share & (X_RING - 1)
-
-    def first_wedge(up, right):
-        return low * (((row + up) & 1) * X_RING + ((column - right * ahead) & (X_RING - 1)))
-
+    core = lax.axis_index("box").astype(jnp.int32) & 1
+    front, back, opposite, row = 1 + 2 * core, 3 - 2 * core, 2, X_RING
+
+    def first_wedge(turn):
+        return low * (share ^ turn)
+
+    soon = (0, row, front, back, row ^ back)
     for k in range(SOON):
-        base = first_wedge(*OFFSETS[k])
+        base = first_wedge(soon[k])
         for i in range(low):
             gathered[base + i] = blocks[k][i]
 
-    far, side, last = [first_wedge(*offset) for offset in OFFSETS[SOON:]]
+    far, side, last = [first_wedge(turn) for turn in (opposite, row ^ front, row ^ opposite)]
     late = jnp.int32(0)
     final = jnp.int32(0)
     per_wedge = slots // mid_count
@@ -399,35 +398,33 @@
     level_one = first_level(leaf_density, phases_first.transpose(1, 0, 2), flat(transfer_first))
     boxes = lax.axis_size("box")
 
-    def moves(up, right):
-        pairs = []
-        for b in range(boxes):
-            for y in range(Y_PAIR):
-                for x in range(X_RING):
-                    side = right if b % 2 == 0 else -right
-                    to_y, to_x = (y + up) % Y_PAIR, (x + side) % X_RING
-                    pairs.append(((b * Y_PAIR + y) * X_RING + x, (b * Y_PAIR + to_y) * X_RING + to_x))
-        return pairs
-
-    def shift(block, up, right):
-        return lax.ppermute(block, ("box", "dir"), moves(up, right))
-
-    other = shift(level_one, 1, 0)
-    front = shift(level_one, 0, 1)
-    back = shift(level_one, 0, -1)
-    far = shift(front, 0, 1)
-    other_front = shift(other, 0, 1)
-    other_back = shift(back, 1, 0)
-    other_far = shift(other_front, 0, 1)
-    blocks = (level_one, other, front, back, other_front)
+    group = lax.axis_size("dir")
+
+    def shift(block, *turns):
+        pairs = [
+            (b * group + d, b * group + (d ^ turns[b % 2]))
+            for b in range(boxes)
+            for d in range(group)
+        ]
+        return lax.ppermute(block, ("box", "dir"), pairs)
+
+    row, front_turns, back_turns = (X_RING, X_RING), (1, 3), (3, 1)
+    other = shift(level_one, *row)
+    back = shift(level_one, *back_turns)
+    front = shift(level_one, *front_turns)
+    other_back = shift(other, *back_turns)
+    far = shift(back, *front_turns)
+    other_front = shift(front, *row)
+    other_far = shift(other_back, *front_turns)
+    blocks = (level_one, other, front, back, other_back)
     switch_trig, top_trig, partial = make_ready(
         phases_switch, phases_top.transpose(1, 0, 2), flat(transfer_switch), level_one
     )
-    weights = make_weights(flat(transfer_switch), back, partial)
+    weights = make_weights(flat(transfer_switch), front, partial)
     most, plan = switch_most(
         child_mid, child_top, blocks, switch_trig, weights, transfer_top.shape[0]
     )
-    late = switch_late(plan, far, other_back, switch_trig, weights, most)
+    late = switch_late(plan, far, other_front, switch_trig, weights, most)
     send = switch_rest(plan, other_far, switch_trig, weights, late, boxes)
     received = lax.all_to_all(send, "box", 0, 0)
     return top_level(received, top_trig, flat(transfer_top))

time: 57.6 us -> 60.1 us (1.043)
  the two profiles are of different devices: /device:TPU:2 before, /device:TPU:4 now
where the time goes in v3:
time: 60.1 us; the launch traced here: 59.9 us
  blocking collectives  28.6 us (48%)
  Pallas kernels  14.2 us (24%)
  starting transfers between devices  8.55 us (14%)
  waiting for transfers between devices  8.36 us (14%)
    all_to_all x1, blocking collectives, upward(): received = lax.all_to_all(send, 'box', 0, 0)  28.6 us
    ppermute x7, starting transfers between devices, shift(): return lax.ppermute(block, ('box', 'dir'), pairs)  8.55 us
    ppermute x7, waiting for transfers between devices, shift(): return lax.ppermute(block, ('box', 'dir'), pairs)  8.36 us
    pallas_call x1, Pallas kernels, switch_most(): pl.pallas_call(functools.partial(most_kernel, top_count), out_shape=(pltp...  3.08 us
    pallas_call x1, Pallas kernels, first_level(): pl.pallas_call(first_kernel, out_shape=pltpu.VMEM((wedges, 16, FULL), jnp...  3.07 us
    pallas_call x1, Pallas kernels, make_ready(): pl.pallas_call(ready_kernel, out_shape=(pltpu.VMEM((2, switch_angles.shap...  2.05 us
    pallas_call x1, Pallas kernels, make_weights(): pl.pallas_call(weights_kernel, out_shape=pltpu.VMEM(weights.shape, jnp.bf...  1.91 us
    pallas_call x1, Pallas kernels, switch_late(): pl.pallas_call(late_kernel, out_shape=pltpu.VMEM(ready.shape, jnp.bfloat1...  1.65 us
  transfers between devices with their start and end apart: 7, of which 3 were waited for; matrix products, arithmetic and copies ran while one was open for 0% of the time, Pallas kernels for 14%

profile of v3, /device:TPU:4, one launch (start us, length us, event | category | flops | bytes accessed | tf_op | source)
XLA Modules:
  0.0 59.9 jit_solution(5721865277999888667)
XLA Ops:
  0.0 3.1 %first_level.1.after.refs_0_ = bf16[12,16,512]{2,1,0:T(8,128)(2,1)S(1)} custom-call(bf16[64,12,8,128]{3,2,1,0:T(8,128)(2,1)} %leaf_hbm.1, f32[12,8,64]{2,1,0:T(8,128)} %bitcast.9, bf16[12,128,512]{2,1,0:T(8,128)(2,1)} %bitcast.8), custom_call_target="tpu_custom_call" | custom-call | tf_op jit(solution)/shard_map/first_level/pallas_call | solution.py:134
  3.1 1.7 %collective-permute-start = (bf16[12,16,512]{2,1,0:T(8,128)(2,1)S(1)}, bf16[12,16,512]{2,1,0:T(8,128)(2,1)S(1)}, u32[]{:S(2)}, u32[]{:S(2)}) collective-permute-start(bf16[12,16,512]{2,1,0:T(8,128)(2,1)S(1)} %first_level.1.after.refs_0_), channel_id=1, source_target_pairs={{0,4},{1,5},{2,6},{3,7},{4,0},{5,1},{6,2},{7,3},{8,12},{9,13},{10,... | collective-permute-start | bytes 589832 | tf_op jit(solution)/shard_map/ppermute | solution.py:409
  4.7 1.2 %collective-permute-start.1 = (bf16[12,16,512]{2,1,0:T(8,128)(2,1)S(1)}, bf16[12,16,512]{2,1,0:T(8,128)(2,1)S(1)}, u32[]{:S(2)}, u32[]{:S(2)}) collective-permute-start(bf16[12,16,512]{2,1,0:T(8,128)(2,1)S(1)} %first_level.1.after.refs_0_), channel_id=1, source_target_pairs={{0,1},{1,0},{2,3},{3,2},{4,5},{5,4},{6,7},{7,6},{8,11},{9,10},{10,... | collective-permute-start | bytes 589832 | tf_op jit(solution)/shard_map/ppermute | solution.py:409
  5.9 0.1 collective-permute-start.2
  6.0 3.8 %collective-permute-done.refs_1_ = bf16[12,16,512]{2,1,0:T(8,128)(2,1)S(1)} collective-permute-done((bf16[12,16,512]{2,1,0:T(8,128)(2,1)S(1)}, bf16[12,16,512]{2,1,0:T(8,128)(2,1)S(1)}, u32[]{:S(2)}, u32[]{:S(2)}) %collective-permute-start) | collective-permute-done | bytes 196640 | tf_op jit(solution)/shard_map/ppermute | solution.py:409
  9.8 0.5 collective-permute-start.3
  10.3 1.0 %collective-permute-done.1.after.refs_2_ = bf16[12,16,512]{2,1,0:T(8,128)(2,1)S(1)} collective-permute-done((bf16[12,16,512]{2,1,0:T(8,128)(2,1)S(1)}, bf16[12,16,512]{2,1,0:T(8,128)(2,1)S(1)}, u32[]{:S(2)}, u32[]{:S(2)}) %collective-permute-start.1) | collective-permute-done | bytes 196640 | tf_op jit(solution)/shard_map/ppermute | solution.py:409
  11.4 0.6 collective-permute-start.6
  11.9 0.0 collective-permute-done.2.refs_3_
  11.9 1.7 %collective-permute-start.5 = (bf16[12,16,512]{2,1,0:T(8,128)(2,1)S(1)}, bf16[12,16,512]{2,1,0:T(8,128)(2,1)S(1)}, u32[]{:S(2)}, u32[]{:S(2)}) collective-permute-start(bf16[12,16,512]{2,1,0:T(8,128)(2,1)S(1)} %collective-permute-done.2.refs_3_), channel_id=1, source_target_pairs={{0,1},{1,0},{2,3},{3,2},{4,5},{5,4},{6,7},{7,6},{8,11},{9,10},{10,... | collective-permute-start | bytes 589832 | tf_op jit(solution)/shard_map/ppermute | solution.py:409
  13.7 3.6 %collective-permute-done.3.refs_4_ = bf16[12,16,512]{2,1,0:T(8,128)(2,1)S(1)} collective-permute-done((bf16[12,16,512]{2,1,0:T(8,128)(2,1)S(1)}, bf16[12,16,512]{2,1,0:T(8,128)(2,1)S(1)}, u32[]{:S(2)}, u32[]{:S(2)}) %collective-permute-start.3) | collective-permute-done | bytes 196640 | tf_op jit(solution)/shard_map/ppermute | solution.py:409
  17.2 2.8 %collective-permute-start.4 = (bf16[12,16,512]{2,1,0:T(8,128)(2,1)S(1)}, bf16[12,16,512]{2,1,0:T(8,128)(2,1)S(1)}, u32[]{:S(2)}, u32[]{:S(2)}) collective-permute-start(bf16[12,16,512]{2,1,0:T(8,128)(2,1)S(1)} %collective-permute-done.3.refs_4_), channel_id=1, source_target_pairs={{0,1},{1,0},{2,3},{3,2},{4,5},{5,4},{6,7},{7,6},{8,11},{9,10},{10,... | collective-permute-start | bytes 589832 | tf_op jit(solution)/shard_map/ppermute | solution.py:409
  20.0 2.0 %make_ready.1 = (f32[2,48,512]{2,1,0:T(8,128)S(1)}, f32[2,6,512]{2,1,0:T(8,128)S(1)}, bf16[48,128,512]{2,1,0:T(8,128)(2,1)S(1)}) custom-call(f32[8,48,64]{2,1,0:T(8,128)} %switch_hbm.1, f32[6,8,64]{2,1,0:T(8,128)} %bitcast.10, bf16[48,128,512]{2,1,0:T(8,128)(2,1)} %bitcast.6, bf16[12,16,512]{2,1,0:T(8,128)(2,1)S(1)} %first_level.1.after.refs_0_), custom_call_target="tpu_custom_call" | custom-call | tf_op jit(solution)/shard_map/make_ready/pallas_call | solution.py:174
  22.0 0.0 copy-start.1
  22.1 0.0 copy-start.2
  22.1 1.9 %make_weights.1.refs_6_.weights = bf16[48,128,512]{2,1,0:T(8,128)(2,1)S(1)} custom-call(bf16[48,128,512]{2,1,0:T(8,128)(2,1)} %bitcast.7, bf16[12,16,512]{2,1,0:T(8,128)(2,1)S(1)} %collective-permute-done.1.after.refs_2_, bf16[48,128,512]{2,1,0:T(8,128)(2,1)S(1)} %get-tuple-element.11.partial), custom_call_target="tpu_custom_call", output_to_operand_aliasing={{}: (2, {})} | custom-call | tf_op jit(solution)/shard_map/make_weights/pallas_call | solution.py:203
  24.0 0.0 copy-done.1
  24.0 0.0 copy-done.2
  24.0 3.1 %switch_most.1 = (bf16[48,8,128]{2,1,0:T(8,128)(2,1)S(1)}, s32[432]{0:T(512)S(1)}) custom-call(s32[48]{0:T(128)S(1)} %copy-done.2, s32[1536]{0:T(1024)S(1)} %copy-done.1, bf16[12,16,512]{2,1,0:T(8,128)(2,1)S(1)} %first_level.1.after.refs_0_, bf16[12,16,512]{2,1,0:T(8,128)(2,1)S(1)} %collective-permute-done.refs_1_, ...), custom_call_target="tpu_custom_call" | custom-call | tf_op jit(solution)/shard_map/switch_most/pallas_call | solution.py:272
  27.1 0.0 collective-permute-done.6.side
  27.1 0.0 collective-permute-done.5.far
  27.1 0.0 copy-start
  27.1 1.6 %switch_late.1.ready = bf16[48,8,128]{2,1,0:T(8,128)(2,1)S(1)} custom-call(s32[432]{0:T(512)S(1)} %get-tuple-element.12.plan, bf16[12,16,512]{2,1,0:T(8,128)(2,1)S(1)} %collective-permute-done.5.far, bf16[12,16,512]{2,1,0:T(8,128)(2,1)S(1)} %collective-permute-done.6.side, f32[2,48,512]{2,1,0:T(8,128)S(1)} %get-tuple-element.10.refs_5_.trig, ...), custom_call_target="tpu_custom_call" | custom-call | tf_op jit(solution)/shard_map/switch_late/pallas_call | solution.py:313
  28.8 0.0 collective-permute-done.4.last
  28.8 1.3 %switch_rest.1 = bf16[32,6,8,128]{3,2,1,0:T(8,128)(2,1)S(1)} custom-call(s32[432]{0:T(512)S(1)} %get-tuple-element.12.plan, bf16[12,16,512]{2,1,0:T(8,128)(2,1)S(1)} %collective-permute-done.4.last, f32[2,48,512]{2,1,0:T(8,128)S(1)} %get-tuple-element.10.refs_5_.trig, bf16[48,128,512]{2,1,0:T(8,128)(2,1)S(1)} %make_weights.1.refs_6_.weights, ...), custom_call_target="tpu_custom_call" | custom-call | tf_op jit(solution)/shard_map/switch_rest/pallas_call | solution.py:340
  30.1 28.6 %all_to_all.5.boxes = bf16[32,6,8,128]{3,2,1,0:T(8,128)(2,1)S(1)} all-to-all(bf16[32,6,8,128]{3,2,1,0:T(8,128)(2,1)S(1)} %switch_rest.1), channel_id=1, replica_groups=mesh['box'=32,'dir'=8] {'box'}, dimensions={0} | all-to-all | bytes 786432 | tf_op jit(solution)/shard_map/all_to_all | solution.py:429
  58.7 0.0 copy-done
  58.7 1.2 %top_level.1 = f32[4,6,8,128]{3,2,1,0:T(8,128)} custom-call(bf16[32,6,8,128]{3,2,1,0:T(8,128)(2,1)S(1)} %all_to_all.5.boxes, f32[2,6,512]{2,1,0:T(8,128)S(1)} %get-tuple-element.14.trig, bf16[6,128,512]{2,1,0:T(8,128)(2,1)S(1)} %bitcast.5), custom_call_target="tpu_custom_call" | custom-call | tf_op jit(solution)/shard_map/top_level/pallas_call | solution.py:373
Async XLA Ops:
  3.1 6.7 %collective-permute-start = (bf16[12,16,512]{2,1,0:T(8,128)(2,1)S(1)}, bf16[12,16,512]{2,1,0:T(8,128)(2,1)S(1)}, u32[]{:S(2)}, u32[]{:S(2)}) collective-permute-start(bf16[12,16,512]{2,1,0:T(8,128)(2,1)S(1)} %first_level.1.after.refs_0_), channel_id=1, source_target_pairs={{0,4},{1,5},{2,6},{3,7},{4,0},{5,1},{6,2},{7,3},{8,12},{9,13},{10,... | collective-permute-start | bytes 589832 | tf_op jit(solution)/shard_map/ppermute | solution.py:409
  4.7 6.6 %collective-permute-start.1 = (bf16[12,16,512]{2,1,0:T(8,128)(2,1)S(1)}, bf16[12,16,512]{2,1,0:T(8,128)(2,1)S(1)}, u32[]{:S(2)}, u32[]{:S(2)}) collective-permute-start(bf16[12,16,512]{2,1,0:T(8,128)(2,1)S(1)} %first_level.1.after.refs_0_), channel_id=1, source_target_pairs={{0,1},{1,0},{2,3},{3,2},{4,5},{5,4},{6,7},{7,6},{8,11},{9,10},{10,... | collective-permute-start | bytes 589832 | tf_op jit(solution)/shard_map/ppermute | solution.py:409
  5.9 6.0 %collective-permute-start.2 = (bf16[12,16,512]{2,1,0:T(8,128)(2,1)S(1)}, bf16[12,16,512]{2,1,0:T(8,128)(2,1)S(1)}, u32[]{:S(2)}, u32[]{:S(2)}) collective-permute-start(bf16[12,16,512]{2,1,0:T(8,128)(2,1)S(1)} %first_level.1.after.refs_0_), channel_id=1, source_target_pairs={{0,3},{1,2},{2,1},{3,0},{4,7},{5,6},{6,5},{7,4},{8,9},{9,8},{10,11... | collective-permute-start | bytes 589832 | tf_op jit(solution)/shard_map/ppermute | solution.py:409
  9.8 7.4 %collective-permute-start.3 = (bf16[12,16,512]{2,1,0:T(8,128)(2,1)S(1)}, bf16[12,16,512]{2,1,0:T(8,128)(2,1)S(1)}, u32[]{:S(2)}, u32[]{:S(2)}) collective-permute-start(bf16[12,16,512]{2,1,0:T(8,128)(2,1)S(1)} %collective-permute-done.refs_1_), channel_id=1, source_target_pairs={{0,3},{1,2},{2,1},{3,0},{4,7},{5,6},{6,5},{7,4},{8,9},{9,8},{10,11... | collective-permute-start | bytes 589832 | tf_op jit(solution)/shard_map/ppermute | solution.py:409
  11.4 15.7 %collective-permute-start.6 = (bf16[12,16,512]{2,1,0:T(8,128)(2,1)S(1)}, bf16[12,16,512]{2,1,0:T(8,128)(2,1)S(1)}, u32[]{:S(2)}, u32[]{:S(2)}) collective-permute-start(bf16[12,16,512]{2,1,0:T(8,128)(2,1)S(1)} %collective-permute-done.1.after.refs_2_), channel_id=1, source_target_pairs={{0,4},{1,5},{2,6},{3,7},{4,0},{5,1},{6,2},{7,3},{8,12},{9,13},{10,... | collective-permute-start | bytes 589832 | tf_op jit(solution)/shard_map/ppermute | solution.py:409
  11.9 15.2 %collective-permute-start.5 = (bf16[12,16,512]{2,1,0:T(8,128)(2,1)S(1)}, bf16[12,16,512]{2,1,0:T(8,128)(2,1)S(1)}, u32[]{:S(2)}, u32[]{:S(2)}) collective-permute-start(bf16[12,16,512]{2,1,0:T(8,128)(2,1)S(1)} %collective-permute-done.2.refs_3_), channel_id=1, source_target_pairs={{0,1},{1,0},{2,3},{3,2},{4,5},{5,4},{6,7},{7,6},{8,11},{9,10},{10,... | collective-permute-start | bytes 589832 | tf_op jit(solution)/shard_map/ppermute | solution.py:409
  17.2 11.6 %collective-permute-start.4 = (bf16[12,16,512]{2,1,0:T(8,128)(2,1)S(1)}, bf16[12,16,512]{2,1,0:T(8,128)(2,1)S(1)}, u32[]{:S(2)}, u32[]{:S(2)}) collective-permute-start(bf16[12,16,512]{2,1,0:T(8,128)(2,1)S(1)} %collective-permute-done.3.refs_4_), channel_id=1, source_target_pairs={{0,1},{1,0},{2,3},{3,2},{4,5},{5,4},{6,7},{7,6},{8,11},{9,10},{10,... | collective-permute-start | bytes 589832 | tf_op jit(solution)/shard_map/ppermute | solution.py:409
  22.0 1.9 %copy-start.1 = (s32[1536]{0:T(1024)S(1)}, s32[1536]{0:T(1024)}, u32[]{:S(2)}) copy-start(s32[1536]{0:T(1024)} %child_top.1) | copy-start | bytes 18436
  22.1 1.9 %copy-start.2 = (s32[48]{0:T(128)S(1)}, s32[48]{0:T(128)}, u32[]{:S(2)}) copy-start(s32[48]{0:T(128)} %child_mid.1) | copy-start | bytes 580
  27.1 31.6 %copy-start = (bf16[6,2,64,512]{3,2,1,0:T(8,128)(2,1)S(1)}, bf16[6,2,64,512]{3,2,1,0:T(8,128)(2,1)}, u32[]{:S(2)}) copy-start(bf16[6,2,64,512]{3,2,1,0:T(8,128)(2,1)} %param.15) | copy-start | bytes 2359300
